TPU v7x, 256 devices: a whole 4x4x8 slice. The times are simulated.
256 devices in a mesh: gx: 16 (over y, x), gy: 4 (over z_lo, core), gz: 4 (over z_hi).
Axes of the slice: x: 4, y: 4, z: 8 (z_hi: 4, z_lo: 2; z = z_hi * 2 + z_lo), core: 2. Of those that a mesh axis runs over, the one named last changes fastest.
Arguments:
- positions: float32 [3, 131072], P(None, ('gx', 'gy', 'gz')), may hold values from 0 to 1
- features: bfloat16 [64, 131072], P(None, ('gx', 'gy', 'gz')), may hold values from -6 to 6
- species: int32 [131072], P(('gx', 'gy', 'gz')), may hold values from 0 to 3
- species_scale: bfloat16 [4], replicated, may hold values from 0.5 to 2
- w_first: bfloat16 [64, 64], replicated, may hold values from -0.75 to 0.75
- w_second: bfloat16 [64, 64], replicated, may hold values from -0.75 to 0.75
- w_radial: float32 [64, 8], replicated, may hold values from -4 to 4
- w_mid: bfloat16 [64, 64], replicated, may hold values from -0.75 to 0.75
- w_last: bfloat16 [64, 64], replicated, may hold values from -0.75 to 0.75
- w_out: float32 [64], replicated, may hold values from -0.75 to 0.75
- ghost_send: int32 [65536], P(('gx', 'gy', 'gz')), may hold values from 0 to 511
- local_first: int32 [5242880], P(('gx', 'gy', 'gz')), may hold values from 0 to 511
- local_second: int32 [5242880], P(('gx', 'gy', 'gz')), may hold values from 0 to 511
- local_mask: int32 [5242880], P(('gx', 'gy', 'gz')), may hold values 0 or 1
- ghost_owner: int32 [3145728], P(('gx', 'gy', 'gz')), may hold values from 0 to 511
- ghost_index: int32 [3145728], P(('gx', 'gy', 'gz')), may hold values from 0 to 1791
- ghost_mask: int32 [3145728], P(('gx', 'gy', 'gz')), may hold values 0 or 1
Outputs:
- forces: float32 [3, 131072], P(None, ('gx', 'gy', 'gz'))
- atom_energy: float32 [131072], P(('gx', 'gy', 'gz'))
Inputs may be any that keep to these rules, and one draw needn't show every extreme that they name: `ghost_send`: rows of the domain's own atoms. `local_first`: owned atoms of the domain. `local_second`: owned atoms of the domain. `ghost_owner`: owned atoms of the domain. `ghost_index`: ghost rows of the domain.
All inputs are finite; a program needn't handle non-finite values. No bound on the sum of `local_mask` or of `ghost_mask` on one device may be relied on, other than what follows from the above.
Results may differ from a plain program's by a relative error of at most 0.0085.
Values may be sent and summed in bfloat16 or wider, within the bound.
A program may use at most 64 MiB of HBM per device.

v0:
```python
import math

import jax
import jax.numpy as jnp
from jax import lax
from jax.sharding import PartitionSpec as P

basis_width = 24.0
domain_edge = 1.0
ghost_offsets = ((1, 0, 0), (0, 1, 0), (0, 0, 1), (1, 1, 0), (1, 0, 1), (0, 1, 1), (1, 1, 1))
scatter_dims = (((1,), (1,)), ((), ()))


def from_behind(value, axis, steps):
    count = lax.axis_size(axis)
    pairs = [(source, (source + steps) % count) for source in range(count)]
    return lax.ppermute(value, axis, pairs)


def pair_energy(squared, left_proj, right_proj, weights, w_radial, w_mid, w_last, w_out):
    basis_count = w_radial.shape[1]
    centers = jnp.arange(basis_count, dtype=jnp.float32) / (basis_count - 1)
    radial_basis = jnp.exp(-basis_width * (squared[None, :] - centers[:, None]) ** 2)
    radial = jnp.dot(
        w_radial, radial_basis, precision=lax.Precision.HIGHEST, preferred_element_type=jnp.float32
    )
    hidden_one = jax.nn.silu(
        left_proj.astype(jnp.float32) + right_proj.astype(jnp.float32) + radial
    ).astype(jnp.bfloat16)
    hidden_two = jax.nn.silu(jnp.dot(w_mid, hidden_one, preferred_element_type=jnp.float32)).astype(
        jnp.bfloat16
    )
    hidden_three = jax.nn.silu(jnp.dot(w_last, hidden_two, preferred_element_type=jnp.float32))
    readout = jnp.dot(
        w_out, hidden_three, precision=lax.Precision.HIGHEST, preferred_element_type=jnp.float32
    )
    envelope = jnp.maximum(1.0 - squared, 0.0) ** 2
    return weights * envelope * readout


def one_hot_cols(rows_in, count):
    return rows_in[None, :] == jnp.arange(count, dtype=jnp.int32)[:, None]


def pair_terms(
    owners,
    partners,
    slot_mask,
    own_table,
    left_all,
    right_table,
    partner_table,
    w_radial,
    w_mid,
    w_last,
    w_out,
):
    total = owners.shape[0]
    own_count = own_table.shape[1]
    partner_count = partner_table.shape[1]
    block_size = math.gcd(total, 2048)
    step_count = total // block_size

    def one_block(carry, pieces):
        owner_sum, partner_sum = carry
        owner_rows, partner_rows, live = pieces
        owner_hot = one_hot_cols(owner_rows, own_count)
        partner_hot = one_hot_cols(partner_rows, partner_count)
        owner_float = owner_hot.astype(jnp.float32)
        partner_float = partner_hot.astype(jnp.float32)
        own_vals = jnp.dot(
            own_table,
            owner_float,
            precision=lax.Precision.HIGHEST,
            preferred_element_type=jnp.float32,
        )
        partner_vals = jnp.dot(
            partner_table,
            partner_float,
            precision=lax.Precision.HIGHEST,
            preferred_element_type=jnp.float32,
        )
        left_proj = jnp.dot(
            left_all, owner_hot.astype(jnp.bfloat16), preferred_element_type=jnp.float32
        ).astype(jnp.bfloat16)
        right_proj = jnp.dot(
            right_table, partner_hot.astype(jnp.bfloat16), preferred_element_type=jnp.float32
        ).astype(jnp.bfloat16)
        displace = partner_vals[:3] - own_vals[:3]
        squared = jnp.sum(displace * displace, axis=0)
        weights = live.astype(jnp.float32) * own_vals[3] * partner_vals[3]

        def energy_of(squared_in):
            return pair_energy(
                squared_in, left_proj, right_proj, weights, w_radial, w_mid, w_last, w_out
            )

        energy, pullback = jax.vjp(energy_of, squared)
        slope = pullback(jnp.ones_like(energy))[0]
        push = 2.0 * displace * slope[None, :]
        owner_vals = jnp.concatenate([push, energy[None, :]], 0)
        owner_sum = owner_sum + lax.dot_general(
            owner_vals,
            owner_float,
            scatter_dims,
            precision=lax.Precision.HIGHEST,
            preferred_element_type=jnp.float32,
        )
        partner_sum = partner_sum + lax.dot_general(
            push,
            partner_float,
            scatter_dims,
            precision=lax.Precision.HIGHEST,
            preferred_element_type=jnp.float32,
        )
        return ((owner_sum, partner_sum), None)

    start = (jnp.zeros((4, own_count), jnp.float32), jnp.zeros((3, partner_count), jnp.float32))
    pieces = (
        owners.reshape(step_count, block_size),
        partners.reshape(step_count, block_size),
        slot_mask.reshape(step_count, block_size),
    )
    sums, unused = lax.scan(one_block, start, pieces)
    return sums


def on_device(
    positions,
    features,
    species,
    species_scale,
    w_first,
    w_second,
    w_radial,
    w_mid,
    w_last,
    w_out,
    ghost_send,
    local_first,
    local_second,
    local_mask,
    ghost_owner,
    ghost_index,
    ghost_mask,
):
    own_count = positions.shape[1]
    send_count = ghost_send.shape[0]
    channels = features.shape[0]
    species_count = species_scale.shape[0]
    onehot = (species[None, :] == jnp.arange(species_count, dtype=jnp.int32)[:, None]).astype(
        species_scale.dtype
    )
    atom_gain = jnp.dot(species_scale, onehot, preferred_element_type=jnp.float32)
    coord_high = positions.astype(jnp.bfloat16)
    coord_low = (positions - coord_high.astype(jnp.float32)).astype(jnp.bfloat16)
    payload = jnp.concatenate(
        [features, coord_high, coord_low, atom_gain.astype(jnp.bfloat16)[None, :]], 0
    )
    send_hot = one_hot_cols(ghost_send, own_count)
    offered = jnp.dot(
        payload, send_hot.astype(jnp.bfloat16), preferred_element_type=jnp.float32
    ).astype(jnp.bfloat16)
    from_z = from_behind(offered, "gz", -1)
    pair_zy = from_behind(jnp.stack([offered, from_z], 1), "gy", -1)
    four_x = from_behind(jnp.stack([offered, from_z, pair_zy[:, 0], pair_zy[:, 1]], 1), "gx", -1)
    blocks = [
        four_x[:, 0],
        pair_zy[:, 0],
        from_z,
        four_x[:, 2],
        four_x[:, 1],
        pair_zy[:, 1],
        four_x[:, 3],
    ]
    own_table = jnp.concatenate([positions, atom_gain[None, :]], 0)
    left_all = jnp.dot(w_first, features, preferred_element_type=jnp.float32).astype(jnp.bfloat16)
    right_own = jnp.dot(w_second, features, preferred_element_type=jnp.float32).astype(jnp.bfloat16)
    local_owner, local_partner = pair_terms(
        local_first,
        local_second,
        local_mask,
        own_table,
        left_all,
        right_own,
        own_table,
        w_radial,
        w_mid,
        w_last,
        w_out,
    )
    ghosts = jnp.stack(blocks, 1).reshape(channels + 7, 7 * send_count)
    shifts = domain_edge * jnp.array(ghost_offsets, dtype=jnp.float32).T
    ghost_feat = ghosts[:channels]
    ghost_high = ghosts[channels : channels + 3].astype(jnp.float32)
    ghost_low = ghosts[channels + 3 : channels + 6].astype(jnp.float32)
    ghost_coords = (
        (ghost_high + ghost_low).reshape(3, 7, send_count) + shifts[:, :, None]
    ).reshape(3, 7 * send_count)
    ghost_gain = ghosts[channels + 6].astype(jnp.float32)
    ghost_table = jnp.concatenate([ghost_coords, ghost_gain[None, :]], 0)
    right_ghost = jnp.dot(w_second, ghost_feat, preferred_element_type=jnp.float32).astype(
        jnp.bfloat16
    )
    ghost_own_sum, ghost_partner = pair_terms(
        ghost_owner,
        ghost_index,
        ghost_mask,
        own_table,
        left_all,
        right_ghost,
        ghost_table,
        w_radial,
        w_mid,
        w_last,
        w_out,
    )
    atom_energy = local_owner[3] + ghost_own_sum[3]
    forces = local_owner[:3] - local_partner + ghost_own_sum[:3]
    ghost_force = -ghost_partner
    slot_forces = ghost_force.reshape(3, 7, send_count)
    upward_z = from_behind(
        jnp.stack([slot_forces[:, 2], slot_forces[:, 4], slot_forces[:, 5], slot_forces[:, 6]], 1),
        "gz",
        1,
    )
    slot_x = slot_forces[:, 0] + upward_z[:, 1]
    slot_y = slot_forces[:, 1] + upward_z[:, 2]
    slot_xy = slot_forces[:, 3] + upward_z[:, 3]
    upward_y = from_behind(jnp.stack([slot_y, slot_xy], 1), "gy", 1)
    upward_x = from_behind(slot_x + upward_y[:, 1], "gx", 1)
    incoming = upward_z[:, 0] + upward_y[:, 0] + upward_x
    forces = forces + lax.dot_general(
        incoming,
        send_hot.astype(jnp.float32),
        scatter_dims,
        precision=lax.Precision.HIGHEST,
        preferred_element_type=jnp.float32,
    )
    return (forces, atom_energy)


def solution(mesh):
    in_specs = (
        P(None, ("gx", "gy", "gz")),
        P(None, ("gx", "gy", "gz")),
        P(("gx", "gy", "gz")),
        P(),
        P(),
        P(),
        P(),
        P(),
        P(),
        P(),
        P(("gx", "gy", "gz")),
        P(("gx", "gy", "gz")),
        P(("gx", "gy", "gz")),
        P(("gx", "gy", "gz")),
        P(("gx", "gy", "gz")),
        P(("gx", "gy", "gz")),
        P(("gx", "gy", "gz")),
    )
    out_specs = (P(None, ("gx", "gy", "gz")), P(("gx", "gy", "gz")))
    return jax.shard_map(
        on_device, mesh=mesh, in_specs=in_specs, out_specs=out_specs, check_vma=False
    )
```

profile of v0, /device:TPU:1, one launch (start us, length us, event | category | flops | bytes accessed | tf_op | source)
XLA Modules:
  0.0 281.9 jit_solution(16773405803951129369)
XLA Ops:
  3.4 6.9 %collective-permute-start = (bf16[71,256]{1,0:T(8,128)(2,1)S(1)}, bf16[71,256]{1,0:T(8,128)(2,1)S(1)}, u32[]{:S(2)}, u32[]{:S(2)}) collective-permute-start(bf16[71,256]{1,0:T(8,128)(2,1)S(1)} %convolution_convert_fusion.7), channel_id=1, source_target_pairs={{0,3},{1,0},{2,1},{3,2},{4,7},{5,4},{6,5},{7,6},{8,11},{9,8},{10,9... | collective-permute-start | bytes 109064 | tf_op jit(solution)/shard_map/ppermute | solution.py:17
  13.0 2.7 collective-permute-done.1
  15.7 5.0 %collective-permute-start.2 = (bf16[71,4,256]{2,0,1:T(8,128)(2,1)S(1)}, bf16[71,4,256]{2,0,1:T(8,128)(2,1)S(1)}, u32[]{:S(2)}, u32[]{:S(2)}) collective-permute-start(bf16[71,4,256]{2,0,1:T(8,128)(2,1)S(1)} %pad_maximum_fusion), channel_id=1, source_target_pairs={{0,240},{16,0},{32,16},{48,32},{64,48},{80,64},{96,80},{112,96},{1... | collective-permute-start | bytes 436232 | tf_op jit(solution)/shard_map/ppermute | solution.py:17
  21.0 3.2 %collective-permute-done.2 = bf16[71,4,256]{2,0,1:T(8,128)(2,1)S(1)} collective-permute-done((bf16[71,4,256]{2,0,1:T(8,128)(2,1)S(1)}, bf16[71,4,256]{2,0,1:T(8,128)(2,1)S(1)}, u32[]{:S(2)}, u32[]{:S(2)}) %collective-permute-start.2) | collective-permute-done | bytes 145440 | tf_op jit(solution)/shard_map/ppermute | solution.py:17
  25.3 126.3 %while.27 = (s32[]{:T(128)}, f32[4,512]{1,0:T(4,128)S(1)}, f32[3,1792]{1,0:T(4,128)S(1)}, s32[6,2048]{1,0:T(8,128)S(1)}, f32[4,1792]{1,0:T(4,128)S(1)}, /*index=...) while((s32[]{:T(128)}, f32[4,512]{1,0:T(4,128)S(1)}, ...), condition=%wide.region_7.8_spmd.clone, body=%wide.region_4.7_spmd.clone.sunk | while | flops 1128016384 | bytes 8792840 | solution.py:124
  26.9 4.6 %fusion.313 = f32[4,2048]{1,0:T(4,128)S(1)} fusion(f32[4,1792]{1,0:T(4,128)S(1)} %get-tuple-element.517, s32[2048]{0:T(1024)S(1)} %bitcast.288), kind=kOutput, calls=%fused_computation.128.clone.1 | convolution fusion | flops 179830784 | bytes 69632 | tf_op jit(solution)/shard_map/while/body/eval_jaxpr/dot_general | solution.py:77
  31.5 2.6 fusion.310
  38.0 6.5 %fusion.320 = f32[3,1792]{1,0:T(4,128)S(1)} fusion(f32[3,2048]{1,0:T(4,128)S(1)} %broadcast_multiply_fusion.5, s32[2048]{0:T(1024)S(1)} %bitcast.290, f32[3,1792]{1,0:T(4,128)S(1)} %get-tuple-element.499, pred[]{:T(512)S(6)} %compare.7), kind=kOutput, calls=%fused_computation.126.clone.1 | convolution fusion | flops 135801344 | bytes 75777 | tf_op jit(solution)/shard_map/while/body/eval_jaxpr/dot_general | solution.py:109
  44.5 1.9 fusion.319
  47.9 4.6 %fusion.313 = f32[4,2048]{1,0:T(4,128)S(1)} fusion(f32[4,1792]{1,0:T(4,128)S(1)} %get-tuple-element.517, s32[2048]{0:T(1024)S(1)} %bitcast.288), kind=kOutput, calls=%fused_computation.128.clone.1 | convolution fusion | flops 179830784 | bytes 69632 | tf_op jit(solution)/shard_map/while/body/eval_jaxpr/dot_general | solution.py:77
  52.5 2.6 fusion.310
  59.0 6.5 %fusion.320 = f32[3,1792]{1,0:T(4,128)S(1)} fusion(f32[3,2048]{1,0:T(4,128)S(1)} %broadcast_multiply_fusion.5, s32[2048]{0:T(1024)S(1)} %bitcast.290, f32[3,1792]{1,0:T(4,128)S(1)} %get-tuple-element.499, pred[]{:T(512)S(6)} %compare.7), kind=kOutput, calls=%fused_computation.126.clone.1 | convolution fusion | flops 135801344 | bytes 75777 | tf_op jit(solution)/shard_map/while/body/eval_jaxpr/dot_general | solution.py:109
  65.5 1.9 fusion.319
  68.9 4.6 %fusion.313 = f32[4,2048]{1,0:T(4,128)S(1)} fusion(f32[4,1792]{1,0:T(4,128)S(1)} %get-tuple-element.517, s32[2048]{0:T(1024)S(1)} %bitcast.288), kind=kOutput, calls=%fused_computation.128.clone.1 | convolution fusion | flops 179830784 | bytes 69632 | tf_op jit(solution)/shard_map/while/body/eval_jaxpr/dot_general | solution.py:77
  73.5 2.6 fusion.310
  80.0 6.5 %fusion.320 = f32[3,1792]{1,0:T(4,128)S(1)} fusion(f32[3,2048]{1,0:T(4,128)S(1)} %broadcast_multiply_fusion.5, s32[2048]{0:T(1024)S(1)} %bitcast.290, f32[3,1792]{1,0:T(4,128)S(1)} %get-tuple-element.499, pred[]{:T(512)S(6)} %compare.7), kind=kOutput, calls=%fused_computation.126.clone.1 | convolution fusion | flops 135801344 | bytes 75777 | tf_op jit(solution)/shard_map/while/body/eval_jaxpr/dot_general | solution.py:109
  86.5 1.9 fusion.319
  89.9 4.6 %fusion.313 = f32[4,2048]{1,0:T(4,128)S(1)} fusion(f32[4,1792]{1,0:T(4,128)S(1)} %get-tuple-element.517, s32[2048]{0:T(1024)S(1)} %bitcast.288), kind=kOutput, calls=%fused_computation.128.clone.1 | convolution fusion | flops 179830784 | bytes 69632 | tf_op jit(solution)/shard_map/while/body/eval_jaxpr/dot_general | solution.py:77
  94.5 2.6 fusion.310
  101.0 6.5 %fusion.320 = f32[3,1792]{1,0:T(4,128)S(1)} fusion(f32[3,2048]{1,0:T(4,128)S(1)} %broadcast_multiply_fusion.5, s32[2048]{0:T(1024)S(1)} %bitcast.290, f32[3,1792]{1,0:T(4,128)S(1)} %get-tuple-element.499, pred[]{:T(512)S(6)} %compare.7), kind=kOutput, calls=%fused_computation.126.clone.1 | convolution fusion | flops 135801344 | bytes 75777 | tf_op jit(solution)/shard_map/while/body/eval_jaxpr/dot_general | solution.py:109
  107.5 1.9 fusion.319
  110.9 4.6 %fusion.313 = f32[4,2048]{1,0:T(4,128)S(1)} fusion(f32[4,1792]{1,0:T(4,128)S(1)} %get-tuple-element.517, s32[2048]{0:T(1024)S(1)} %bitcast.288), kind=kOutput, calls=%fused_computation.128.clone.1 | convolution fusion | flops 179830784 | bytes 69632 | tf_op jit(solution)/shard_map/while/body/eval_jaxpr/dot_general | solution.py:77
  115.5 2.6 fusion.310
  122.0 6.5 %fusion.320 = f32[3,1792]{1,0:T(4,128)S(1)} fusion(f32[3,2048]{1,0:T(4,128)S(1)} %broadcast_multiply_fusion.5, s32[2048]{0:T(1024)S(1)} %bitcast.290, f32[3,1792]{1,0:T(4,128)S(1)} %get-tuple-element.499, pred[]{:T(512)S(6)} %compare.7), kind=kOutput, calls=%fused_computation.126.clone.1 | convolution fusion | flops 135801344 | bytes 75777 | tf_op jit(solution)/shard_map/while/body/eval_jaxpr/dot_general | solution.py:109
  128.5 1.9 fusion.319
  131.9 4.6 %fusion.313 = f32[4,2048]{1,0:T(4,128)S(1)} fusion(f32[4,1792]{1,0:T(4,128)S(1)} %get-tuple-element.517, s32[2048]{0:T(1024)S(1)} %bitcast.288), kind=kOutput, calls=%fused_computation.128.clone.1 | convolution fusion | flops 179830784 | bytes 69632 | tf_op jit(solution)/shard_map/while/body/eval_jaxpr/dot_general | solution.py:77
  136.5 2.6 fusion.310
  143.0 6.5 %fusion.320 = f32[3,1792]{1,0:T(4,128)S(1)} fusion(f32[3,2048]{1,0:T(4,128)S(1)} %broadcast_multiply_fusion.5, s32[2048]{0:T(1024)S(1)} %bitcast.290, f32[3,1792]{1,0:T(4,128)S(1)} %get-tuple-element.499, pred[]{:T(512)S(6)} %compare.7), kind=kOutput, calls=%fused_computation.126.clone.1 | convolution fusion | flops 135801344 | bytes 75777 | tf_op jit(solution)/shard_map/while/body/eval_jaxpr/dot_general | solution.py:109
  149.5 1.9 fusion.319
  153.7 3.4 %collective-permute-done.3 = f32[3,4,256]{2,0,1:T(4,128)S(1)} collective-permute-done((f32[3,4,256]{2,0,1:T(4,128)S(1)}, f32[3,4,256]{2,0,1:T(4,128)S(1)}, u32[]{:S(2)}, u32[]{:S(2)}) %collective-permute-start.3) | collective-permute-done | bytes 12320 | tf_op jit(solution)/shard_map/ppermute | solution.py:17
  158.8 115.4 %while.26 = (s32[]{:T(128)}, f32[4,512]{1,0:T(4,128)S(1)}, f32[3,512]{1,0:T(4,128)S(1)}, s32[10,2048]{1,0:T(8,128)S(1)}, f32[4,512]{1,0:T(4,128)S(1)}, /*index=5...) while((s32[]{:T(128)}, f32[4,512]{1,0:T(4,128)S(1)}, ...), condition=%wide.region_3.4_spmd.clone, body=%wide.region_0.3_spmd.clone.sunk | while | flops 564399104 | bytes 8577792 | solution.py:124
  275.0 6.0 %collective-permute-done.5 = f32[3,256]{1,0:T(4,128)S(1)} collective-permute-done((f32[3,256]{1,0:T(4,128)S(1)}, f32[3,256]{1,0:T(4,128)S(1)}, u32[]{:S(2)}, u32[]{:S(2)}) %collective-permute-start.5) | collective-permute-done | bytes 3104 | tf_op jit(solution)/shard_map/ppermute | solution.py:17
  (364 shorter events, 158.6 us)
Async XLA Ops:
  0.6 24.4 %copy-start = (bf16[64,64]{1,0:T(8,128)(2,1)S(1)}, bf16[64,64]{1,0:T(8,128)(2,1)}, u32[]{:S(2)}) copy-start(bf16[64,64]{1,0:T(8,128)(2,1)} %param.27) | copy-start | bytes 24580
  0.6 20.1 %copy-start.2 = (bf16[64,512]{1,0:T(8,128)(2,1)S(1)}, bf16[64,512]{1,0:T(8,128)(2,1)}, u32[]{:S(2)}) copy-start(bf16[64,512]{1,0:T(8,128)(2,1)} %param.23) | copy-start | bytes 196612
  0.7 20.0 %copy-start.10 = (bf16[64,64]{1,0:T(8,128)(2,1)S(1)}, bf16[64,64]{1,0:T(8,128)(2,1)}, u32[]{:S(2)}) copy-start(bf16[64,64]{1,0:T(8,128)(2,1)} %param.26) | copy-start | bytes 24580
  2.3 18.6 %copy-start.6 = (s32[12288]{0:T(1024)S(1)}, s32[12288]{0:T(1024)}, u32[]{:S(2)}) copy-start(s32[12288]{0:T(1024)} %param.37) | copy-start | bytes 147460
  2.3 18.6 %copy-start.7 = (s32[12288]{0:T(1024)S(1)}, s32[12288]{0:T(1024)}, u32[]{:S(2)}) copy-start(s32[12288]{0:T(1024)} %param.36) | copy-start | bytes 147460
  3.4 17.5 %copy-start.8 = (s32[12288]{0:T(1024)S(1)}, s32[12288]{0:T(1024)}, u32[]{:S(2)}) copy-start(s32[12288]{0:T(1024)} %param.38) | copy-start | bytes 147460
  3.4 17.6 %copy-start.9 = (f32[3,512]{1,0:T(4,128)S(1)}, f32[3,512]{1,0:T(4,128)}, u32[]{:S(2)}) copy-start(f32[3,512]{1,0:T(4,128)} %param.22) | copy-start | bytes 18436
  3.4 8.0 %collective-permute-start = (bf16[71,256]{1,0:T(8,128)(2,1)S(1)}, bf16[71,256]{1,0:T(8,128)(2,1)S(1)}, u32[]{:S(2)}, u32[]{:S(2)}) collective-permute-start(bf16[71,256]{1,0:T(8,128)(2,1)S(1)} %convolution_convert_fusion.7), channel_id=1, source_target_pairs={{0,3},{1,0},{2,1},{3,2},{4,7},{5,4},{6,5},{7,6},{8,11},{9,8},{10,9... | collective-permute-start | bytes 109064 | tf_op jit(solution)/shard_map/ppermute | solution.py:17
  11.4 4.3 %collective-permute-start.1 = (bf16[71,2,256]{2,0,1:T(8,128)(2,1)S(1)}, bf16[71,2,256]{2,0,1:T(8,128)(2,1)S(1)}, u32[]{:S(2)}, u32[]{:S(2)}) collective-permute-start(bf16[71,2,256]{2,0,1:T(8,128)(2,1)S(1)} %pad_maximum_fusion.1), channel_id=1, source_target_pairs={{0,12},{4,0},{8,4},{12,8},{1,13},{5,1},{9,5},{13,9},{2,14},{6,2},{... | collective-permute-start | bytes 218120 | tf_op jit(solution)/shard_map/ppermute | solution.py:17
  15.7 8.5 %collective-permute-start.2 = (bf16[71,4,256]{2,0,1:T(8,128)(2,1)S(1)}, bf16[71,4,256]{2,0,1:T(8,128)(2,1)S(1)}, u32[]{:S(2)}, u32[]{:S(2)}) collective-permute-start(bf16[71,4,256]{2,0,1:T(8,128)(2,1)S(1)} %pad_maximum_fusion), channel_id=1, source_target_pairs={{0,240},{16,0},{32,16},{48,32},{64,48},{80,64},{96,80},{112,96},{1... | collective-permute-start | bytes 436232 | tf_op jit(solution)/shard_map/ppermute | solution.py:17
  24.2 0.7 copy-start.11
  24.3 0.9 copy-start.1
  24.3 0.9 copy-start.12
  24.3 0.9 copy-start.13
  24.3 0.9 copy-start.15
  25.3 128.4 %copy-start.3 = (s32[20480]{0:T(1024)S(1)}, s32[20480]{0:T(1024)}, u32[]{:S(2)}) copy-start(s32[20480]{0:T(1024)} %param.34) | copy-start | bytes 245764
  151.6 2.1 copy-start.4
  151.6 2.1 copy-start.5
  151.7 5.5 %collective-permute-start.3 = (f32[3,4,256]{2,0,1:T(4,128)S(1)}, f32[3,4,256]{2,0,1:T(4,128)S(1)}, u32[]{:S(2)}, u32[]{:S(2)}) collective-permute-start(f32[3,4,256]{2,0,1:T(4,128)S(1)} %pad_maximum_fusion.3), channel_id=1, source_target_pairs={{0,1},{1,2},{2,3},{3,0},{4,5},{5,6},{6,7},{7,4},{8,9},{9,10},{10,1... | collective-permute-start | bytes 36872 | tf_op jit(solution)/shard_map/ppermute | solution.py:17
  157.1 117.1 %collective-permute-start.4 = (f32[3,2,256]{2,0,1:T(4,128)S(1)}, f32[3,2,256]{2,0,1:T(4,128)S(1)}, u32[]{:S(2)}, u32[]{:S(2)}) collective-permute-start(f32[3,2,256]{2,0,1:T(4,128)S(1)} %pad_maximum_fusion.5), channel_id=1, source_target_pairs={{0,4},{4,8},{8,12},{12,0},{1,5},{5,9},{9,13},{13,1},{2,6},{6,10},{... | collective-permute-start | bytes 18440 | tf_op jit(solution)/shard_map/ppermute | solution.py:17
  158.8 122.2 %copy-start.14 = (s32[256]{0:T(256)S(1)}, s32[256]{0:T(256)}, u32[]{:S(2)}) copy-start(s32[256]{0:T(256)} %param.32) | copy-start | bytes 3076
  274.3 6.6 %collective-permute-start.5 = (f32[3,256]{1,0:T(4,128)S(1)}, f32[3,256]{1,0:T(4,128)S(1)}, u32[]{:S(2)}, u32[]{:S(2)}) collective-permute-start(f32[3,256]{1,0:T(4,128)S(1)} %bitcast.299), channel_id=1, source_target_pairs={{0,16},{16,32},{32,48},{48,64},{64,80},{80,96},{96,112},{112,128},... | collective-permute-start | bytes 9224 | tf_op jit(solution)/shard_map/ppermute | solution.py:17
where the time goes:
time: 282 us
  matrix products  241 us (85%)
  starting transfers between devices  17.1 us (6%)
  waiting for transfers between devices  16.2 us (6%)
  other arithmetic  3.2 us (1%)
    dot_general x16, matrix products, one_block(): lax.dot_general(push, partner_float, scatter_dims, precision=lax.Precisio...  58.3 us
    dot_general x16, matrix products, one_block(): jnp.dot(partner_table, partner_float, precision=lax.Precision.HIGHEST, pr...  41.2 us
    dot_general x16, matrix products, one_block(): lax.dot_general(owner_vals, owner_float, scatter_dims, precision=lax.Prec...  31.2 us
    dot_general x16, matrix products, one_block(): jnp.dot(right_table, partner_hot.astype(jnp.bfloat16), preferred_element_...  24 us
    dot_general x16, matrix products, one_block(): jnp.dot(own_table, owner_float, precision=lax.Precision.HIGHEST, preferre...  22.1 us
    dot_general x32, matrix products, pair_energy(): jnp.dot(w_radial, radial_basis, precision=lax.Precision.HIGHEST, preferre...  19.5 us
    ppermute x6, starting transfers between devices, from_behind(): return lax.ppermute(value, axis, pairs)  17.1 us
    ppermute x6, waiting for transfers between devices, from_behind(): return lax.ppermute(value, axis, pairs)  16.2 us
  transfers between devices with their start and end apart: 6, of which 5 were waited for; matrix products, arithmetic and copies ran while one was open for 41% of the time, Pallas kernels for 0%

commit v1 on v0

v1 whole, which is shorter than its diff:
```python
import jax
import jax.numpy as jnp
from jax import lax
from jax.experimental import pallas as pl
from jax.experimental.pallas import tpu as pltpu
from jax.sharding import PartitionSpec as P

OFFSETS = ((1, 0, 0), (0, 1, 0), (0, 0, 1), (1, 1, 0), (1, 0, 1), (0, 1, 1), (1, 1, 1))
MESH_IDS = pl.DeviceIdType.MESH
VMEM = pl.BlockSpec(memory_space=pltpu.VMEM)
NT = (((1,), (1,)), ((), ()))
WIDTH = 24.0
F32, BF16, I32 = jnp.float32, jnp.bfloat16, jnp.int32
LIVE = 128
ROWS = 80


def neighbour(offset, sign):
    where = []
    for axis, step in zip(("gx", "gy", "gz"), offset):
        count = lax.axis_size(axis)
        where.append(lax.rem(lax.axis_index(axis) + sign * step + count, count))
    return tuple(where)


def meet(sign):
    barrier = pltpu.get_barrier_semaphore()
    for offset in OFFSETS:
        pl.semaphore_signal(barrier, inc=1, device_id=neighbour(offset, sign), device_id_type=MESH_IDS)
    return barrier


def one_hot(row, count):
    levels = lax.broadcasted_iota(jnp.int16, (count, row.shape[1]), 0)
    return jnp.where(levels == row.astype(jnp.int16), jnp.ones((), BF16), jnp.zeros((), BF16))


def split_two(value):
    high = value.astype(BF16).astype(F32)
    return high, value - high


def offer_kernel(pos_ref, feat_ref, species_ref, scale_ref, first_ref, second_ref, send_ref,
                 own_ref, tables_ref, ghost_ref, offered, send_sem, recv_sem):
    barrier = meet(1)
    pos = pos_ref[...]
    species = species_ref[...]
    scale = scale_ref[...].astype(F32)
    gain = jnp.zeros(species.shape, F32)
    for kind in range(scale.shape[1]):
        gain = jnp.where(species == kind, scale[:, kind:kind + 1], gain)
    count = pos.shape[1]
    own_ref[0:3, :] = pos
    own_ref[3:4, :] = gain
    own_ref[4:8, :] = jnp.zeros((4, count), F32)
    feat = feat_ref[...]
    right = (jnp.dot(second_ref[...], feat, preferred_element_type=F32).astype(BF16).astype(F32) * 0.5).astype(BF16)
    high = pos.astype(BF16).astype(F32)
    tail = jnp.concatenate([high, pos - high, gain, jnp.zeros((9, count), F32)], 0).astype(BF16)
    payload = jnp.concatenate([right, tail], 0)
    hot = one_hot(send_ref[...], count)
    offered[...] = jnp.dot(payload, hot, preferred_element_type=F32).astype(BF16)
    pl.semaphore_wait(barrier, len(OFFSETS))
    copies = []
    for k, offset in enumerate(OFFSETS):
        copy = pltpu.make_async_remote_copy(
            src_ref=offered, dst_ref=ghost_ref.at[k], send_sem=send_sem.at[k], recv_sem=recv_sem.at[k],
            device_id=neighbour(offset, -1), device_id_type=MESH_IDS)
        copy.start()
        copies.append(copy)
    left = (jnp.dot(first_ref[...], feat, preferred_element_type=F32).astype(BF16).astype(F32) * 0.5).astype(BF16)
    tables_ref[:, 0:count] = left
    tables_ref[:, count:2 * count] = right
    for copy in copies:
        copy.wait()


def home_kernel(sums_ref, ghost_ref, send_ref, force_ref, energy_ref, arrived, send_sem, recv_sem):
    barrier = meet(-1)
    pl.semaphore_wait(barrier, len(OFFSETS))
    copies = []
    for k, offset in enumerate(OFFSETS):
        copy = pltpu.make_async_remote_copy(
            src_ref=ghost_ref.at[k], dst_ref=arrived.at[k], send_sem=send_sem.at[k], recv_sem=recv_sem.at[k],
            device_id=neighbour(offset, 1), device_id_type=MESH_IDS)
        copy.start()
        copies.append(copy)
    sums = sums_ref[...]
    count = sums.shape[1]
    energy_ref[...] = sums[3:4, :]
    hot = one_hot(send_ref[...], count)
    for copy in copies:
        copy.wait()
    total = arrived[0]
    for k in range(1, len(OFFSETS)):
        total = total + arrived[k]
    high, rest = split_two(total)
    mid, low = split_two(rest)
    parts = jnp.concatenate([high, mid, low, jnp.zeros_like(low)], 0).astype(BF16)
    back = lax.dot_general(parts, hot, NT, preferred_element_type=F32)
    back = back[0:8] + back[8:16] + back[16:24]
    force_ref[...] = sums[0:3, :] - back[0:3, :]


def take_lanes(table, index):
    return jnp.take_along_axis(table, index, axis=1, mode="promise_in_bounds")


def pairs_kernel(own_ref, tables_ref, ghost_ref, first_ref, second_ref, lmask_ref, gowner_ref, gindex_ref, gmask_ref,
                 radial_ref, mid_ref, last_ref, out_ref, sums_ref, gforce_ref,
                 own_tab, ghost_tab, gtable, words, live, ranks, packed, hot_own, hot_par, quant, back,
                 acc_own, acc_loc, acc_gho):
    count = own_ref.shape[1]
    chunks = count // 128
    blocks = len(OFFSETS)
    sends = ghost_ref.shape[2]
    gchunks = blocks * sends // 128
    lrows, grows = first_ref.shape[0], gowner_ref.shape[0]
    lane = lax.broadcasted_iota(I32, (8, 128), 1)

    for c in range(4):
        for ch in range(chunks):
            own_tab[c * chunks + ch] = jnp.broadcast_to(own_ref[c:c + 1, 128 * ch:128 * ch + 128], (8, 128))
    for k, offset in enumerate(OFFSETS):
        gtable[:, sends * k:sends * (k + 1)] = ghost_ref[k, 0:64, :]
        tail = ghost_ref[k, 64:80, :].astype(F32)
        for c in range(4):
            row = tail[c:c + 1] + tail[c + 3:c + 4] + float(offset[c]) if c < 3 else tail[6:7]
            for half in range(sends // 128):
                ghost_tab[c * gchunks + k * (sends // 128) + half] = jnp.broadcast_to(row[:, 128 * half:128 * half + 128], (8, 128))

    def pick(tab, n, c, low, high):
        value = take_lanes(tab[c * n], low)
        for ch in range(1, n):
            value = jnp.where(high == ch, take_lanes(tab[c * n + ch], low), value)
        return value

    def geometry(own, partner, tab, n):
        low_i, high_i, low_j, high_j = own & 127, own >> 7, partner & 127, partner >> 7
        gap = [pick(tab, n, c, low_j, high_j) - pick(own_tab, chunks, c, low_i, high_i) for c in range(3)]
        return gap, gap[0] * gap[0] + gap[1] * gap[1] + gap[2] * gap[2]

    for base, rows, own_list, par_list, mask_list, tab, n in (
        (0, lrows, first_ref, second_ref, lmask_ref, own_tab, chunks),
        (lrows, grows, gowner_ref, gindex_ref, gmask_ref, ghost_tab, gchunks),
    ):
        def find(v, carry, base=base, own_list=own_list, par_list=par_list, mask_list=mask_list, tab=tab, n=n):
            at = pl.ds(pl.multiple_of(8 * v, 8), 8)
            own, partner = own_list[at, :], par_list[at, :]
            gap, squared = geometry(own, partner, tab, n)
            alive = jnp.logical_and(mask_list[at, :] > 0, squared < 1.0)
            to = pl.ds(pl.multiple_of(base + 8 * v, 8), 8)
            live[to, :] = jnp.where(alive, 1.0, 0.0)
            words[to, :] = jnp.where(alive, (own << 8) + (partner << 17) + LIVE, 0)
            return carry
        lax.fori_loop(0, rows // 8, find, 0, unroll=4)

    above = jnp.where(lax.broadcasted_iota(I32, (128, 128), 0) < lax.broadcasted_iota(I32, (128, 128), 1), 1.0, 0.0)
    adder = jnp.concatenate([above, jnp.ones((128, 128), F32)], 1).astype(BF16)
    ranks[...] = jnp.dot(live[...].astype(BF16), adder, preferred_element_type=F32)

    trips = []
    for base, rows in ((0, lrows), (lrows, grows)):
        tiles = rows // 8
        stand = jnp.zeros((8, 128), I32)
        slots = [jnp.zeros((8, 128), I32) for _ in range(tiles)]
        for v in range(tiles):
            at = slice(base + 8 * v, base + 8 * v + 8)
            word = words[at, :]
            rank = ranks[at, 0:128].astype(I32)
            number = ranks[at, 128:256].astype(I32)
            word = jnp.where(word > 0, word + (lane - rank), 0)
            for bit in range(7):
                moved = pltpu.roll(word, 128 - (1 << bit), 1)
                stay = jnp.where((word & (1 << bit)) > 0, 0, word)
                word = jnp.where((moved & (1 << bit)) > 0, moved, stay)
            turn = (lane - stand) & 127
            word = take_lanes(word, turn)
            row = jnp.where(turn < number, (stand + turn) >> 7, -1)
            for t in range(v + 1):
                slots[t] = jnp.where(row == t, word, slots[t])
            stand = stand + number
        for t in range(tiles):
            packed[base + 8 * t:base + 8 * t + 8, :] = slots[t]
        trips.append((jnp.max(stand) + 127) >> 7)

    acc_own[...] = jnp.zeros_like(acc_own)
    acc_loc[...] = jnp.zeros_like(acc_loc)
    acc_gho[...] = jnp.zeros_like(acc_gho)

    w_mid = (mid_ref[...].astype(F32) * 0.5).astype(BF16)
    w_last = (last_ref[...].astype(F32) * 0.5).astype(BF16)
    radial_high, radial_low = split_two(radial_ref[...] * 0.5)
    nb = radial_ref.shape[1]
    spot = lax.broadcasted_iota(I32, (nb, 4 * nb), 1)
    term = lax.broadcasted_iota(I32, (nb, 4 * nb), 0)
    place_high = jnp.where((spot == term) | (spot == term + nb), 1.0, 0.0).astype(BF16)
    place_low = jnp.where(spot == term + 2 * nb, 1.0, 0.0).astype(BF16)
    w_radial = (jnp.dot(radial_high.astype(BF16), place_high, preferred_element_type=F32)
                + jnp.dot(radial_low.astype(BF16), place_low, preferred_element_type=F32)).astype(BF16)
    channels = mid_ref.shape[0]
    eye = lax.broadcasted_iota(I32, (channels, channels), 0) == lax.broadcasted_iota(I32, (channels, channels), 1)
    w_out = jnp.sum(jnp.where(eye, jnp.broadcast_to(out_ref[...], (channels, channels)), 0.0), 1, keepdims=True)
    centers = lax.broadcasted_iota(I32, (nb, 128), 0).astype(F32) / (nb - 1)

    def activate(y, tangent):
        up = 1.0 + jnp.tanh(y)
        value = y * up
        return value, (up + value * (2.0 - up)) * tangent

    for base, tab, n, acc_par, is_ghost in ((0, own_tab, chunks, acc_loc, False), (lrows, ghost_tab, gchunks, acc_gho, True)):
        def step(t, carry, base=base, tab=tab, n=n, acc_par=acc_par, is_ghost=is_ghost):
            word = packed[pl.ds(pl.multiple_of(base + 8 * t, 8), 8), :]
            own, partner = (word >> 8) & 511, word >> 17
            low_i, high_i, low_j, high_j = own & 127, own >> 7, partner & 127, partner >> 7
            gap, squared = geometry(own, partner, tab, n)
            weight = jnp.where((word & LIVE) > 0, pick(own_tab, chunks, 3, low_i, high_i) * pick(tab, n, 3, low_j, high_j), 0.0)
            reads, slopes = [], []
            for half in range(4):
                pair = (2 * half, 2 * half + 1)
                wide = lambda x: jnp.concatenate([x[r:r + 1] for r in pair], 1)
                li, hi, lj, hj = wide(low_i), wide(high_i), wide(low_j), wide(high_j)
                cols = slice(256 * half, 256 * half + 256)
                ho, hp = one_hot(li, 128), one_hot(lj, 128)
                hot_own[:, cols] = ho
                hot_par[:, cols] = hp
                zero = jnp.zeros((), BF16)
                hi_b = jnp.broadcast_to(hi.astype(jnp.int16), (128, 256))
                hj_b = jnp.broadcast_to(hj.astype(jnp.int16), (128, 256))
                hots_i = jnp.concatenate([jnp.where(hi_b == jnp.int16(ch), ho, zero) for ch in range(chunks)], 0)
                hots_j = jnp.concatenate([jnp.where(hj_b == jnp.int16(ch), hp, zero) for ch in range(n)], 0)
                tiles, slants = [], []
                for r in pair:
                    off = squared[r:r + 1] - centers
                    basis = jnp.exp(-WIDTH * off * off)
                    tiles.append(basis)
                    slants.append((-2.0 * WIDTH) * off * basis)
                both = jnp.concatenate(tiles + slants, 1)
                high, low = split_two(both)
                stack = jnp.concatenate([high, low, high, jnp.zeros_like(low)], 0).astype(BF16)
                radial = jnp.dot(w_radial, stack, preferred_element_type=F32)
                if is_ghost:
                    gathered = jnp.dot(tables_ref[:, 0:count], hots_i, preferred_element_type=F32) + jnp.dot(
                        gtable[...], hots_j, preferred_element_type=F32)
                else:
                    gathered = jnp.dot(tables_ref[...], jnp.concatenate([hots_i, hots_j], 0), preferred_element_type=F32)
                value, slope = activate(gathered + radial[:, 0:256], radial[:, 256:512])
                for w in (w_mid, w_last):
                    mixed = jnp.dot(w, jnp.concatenate([value, slope], 1).astype(BF16), preferred_element_type=F32)
                    value, slope = activate(mixed[:, 0:256], mixed[:, 256:512])
                reads.append(jnp.sum(value * w_out, 0, keepdims=True))
                slopes.append(jnp.sum(slope * w_out, 0, keepdims=True))
            tall = lambda xs: jnp.concatenate([x[:, 128 * k:128 * k + 128] for x in xs for k in range(2)], 0)
            readout, reslope = tall(reads), tall(slopes)
            near = jnp.maximum(1.0 - squared, 0.0)
            envelope = near * near
            energy = weight * envelope * readout
            slope = weight * (envelope * reslope - 2.0 * near * readout)
            outs = [2.0 * g * slope for g in gap] + [energy]
            splits = [split_two(x) for x in outs]
            for q in range(4):
                quant[8 * q:8 * q + 8, :] = splits[q][0]
                quant[32 + 8 * q:40 + 8 * q, :] = splits[q][1]
            a_own, a_par = [], []
            for r in range(8):
                tile = quant[pl.ds(r, 8, stride=8), :]
                a_own.append(jnp.concatenate([jnp.where(high_i[r:r + 1] == ch, tile, 0.0) for ch in range(chunks)], 0))
                a_par.append(jnp.concatenate([jnp.where(high_j[r:r + 1] == ch, tile, 0.0) for ch in range(n)], 0))
            acc_own[...] += lax.dot_general(jnp.concatenate(a_own, 1).astype(BF16), hot_own[...], NT, preferred_element_type=F32)
            acc_par[...] += lax.dot_general(jnp.concatenate(a_par, 1).astype(BF16), hot_par[...], NT, preferred_element_type=F32)
            return carry
        lax.fori_loop(0, trips[1 if is_ghost else 0], step, 0)

    for ch in range(chunks):
        own = acc_own[8 * ch:8 * ch + 4, :] + acc_own[8 * ch + 4:8 * ch + 8, :]
        loc = acc_loc[8 * ch:8 * ch + 4, :] + acc_loc[8 * ch + 4:8 * ch + 8, :]
        cols = slice(128 * ch, 128 * ch + 128)
        sums_ref[0:3, cols] = own[0:3] - loc[0:3]
        sums_ref[3:4, cols] = own[3:4]
        sums_ref[4:8, cols] = jnp.zeros((4, 128), F32)
    per = sends // 128
    for ch in range(gchunks):
        cols = slice(128 * (ch % per), 128 * (ch % per) + 128)
        gforce_ref[ch // per, 0:4, cols] = acc_gho[8 * ch:8 * ch + 4, :] + acc_gho[8 * ch + 4:8 * ch + 8, :]
        gforce_ref[ch // per, 4:8, cols] = jnp.zeros((4, 128), F32)


def call_pairs(own, tables, ghosts, first, second, lmask, gowner, gindex, gmask, w_radial, w_mid, w_last, w_out):
    count = own.shape[1]
    channels = w_mid.shape[0]
    gcount = len(OFFSETS) * ghosts.shape[2]
    total = first.shape[0] + gowner.shape[0]
    chunks, gchunks = count // 128, gcount // 128
    v = pltpu.VMEM
    return pl.pallas_call(
        pairs_kernel,
        name="pairs",
        out_shape=(jax.ShapeDtypeStruct((8, count), F32),
                   jax.ShapeDtypeStruct((len(OFFSETS), 8, ghosts.shape[2]), F32)),
        in_specs=[VMEM] * 13,
        out_specs=(VMEM, VMEM),
        scratch_shapes=[
            v((4 * chunks, 8, 128), F32), v((4 * gchunks, 8, 128), F32), v((channels, gcount), BF16),
            v((total, 128), I32), v((total, 128), F32), v((total, 256), F32), v((total, 128), I32),
            v((128, 1024), BF16), v((128, 1024), BF16), v((64, 128), F32), v((8, 128), F32),
            v((8 * chunks, 128), F32), v((8 * chunks, 128), F32), v((8 * gchunks, 128), F32),
        ],
        compiler_params=pltpu.CompilerParams(vmem_limit_bytes=48 << 20),
    )(own, tables, ghosts, first, second, lmask, gowner, gindex, gmask, w_radial, w_mid, w_last, w_out)


def on_device(positions, features, species, species_scale, w_first, w_second, w_radial, w_mid, w_last, w_out,
              ghost_send, local_first, local_second, local_mask, ghost_owner, ghost_index, ghost_mask):
    count = positions.shape[1]
    sends = ghost_send.shape[0]
    channels = features.shape[0]
    blocks = len(OFFSETS)
    send_row = ghost_send.reshape(1, sends)
    own, tables, ghosts = pl.pallas_call(
        offer_kernel,
        name="offer",
        out_shape=(jax.ShapeDtypeStruct((8, count), F32),
                   jax.ShapeDtypeStruct((channels, 2 * count), BF16),
                   jax.ShapeDtypeStruct((blocks, ROWS, sends), BF16)),
        in_specs=[VMEM] * 7,
        out_specs=(VMEM, VMEM, VMEM),
        scratch_shapes=[pltpu.VMEM((ROWS, sends), BF16), pltpu.SemaphoreType.DMA((blocks,)), pltpu.SemaphoreType.DMA((blocks,))],
        compiler_params=pltpu.CompilerParams(collective_id=0, has_side_effects=True),
    )(positions, features, species.reshape(1, count), species_scale.reshape(1, -1), w_first, w_second, send_row)
    lists = [x.reshape(-1, 128) for x in (local_first, local_second, local_mask, ghost_owner, ghost_index, ghost_mask)]
    sums, gforce = call_pairs(own, tables, ghosts, *lists, w_radial, w_mid, w_last, w_out.reshape(1, channels))
    forces, energy = pl.pallas_call(
        home_kernel,
        name="home",
        out_shape=(jax.ShapeDtypeStruct((3, count), F32), jax.ShapeDtypeStruct((1, count), F32)),
        in_specs=[VMEM] * 3,
        out_specs=(VMEM, VMEM),
        scratch_shapes=[pltpu.VMEM((blocks, 8, sends), F32), pltpu.SemaphoreType.DMA((blocks,)), pltpu.SemaphoreType.DMA((blocks,))],
        compiler_params=pltpu.CompilerParams(collective_id=1, has_side_effects=True),
    )(sums, gforce, send_row)
    return forces, energy.reshape(count)


def solution(mesh):
    everywhere = ("gx", "gy", "gz")
    wide, flat, copied = P(None, everywhere), P(everywhere), P()
    in_specs = (wide, wide, flat) + (copied,) * 7 + (flat,) * 7
    return jax.shard_map(on_device, mesh=mesh, in_specs=in_specs, out_specs=(wide, flat), check_vma=False)
```

time: 282 us -> 98 us (0.35)
  matrix products: 241 us -> 0 us
  Pallas kernels: 0 us -> 84.8 us
  starting transfers between devices: 17.1 us -> 0 us
  waiting for transfers between devices: 16.2 us -> 0 us
  local copies, waits for them, and re-layouts: 1.49 us -> 11.8 us
  other arithmetic: 3.2 us -> 0 us
    dot_general x198 -> x0, matrix products: 241 us -> none  [the longest x16 58.3 us: one_block(): lax.dot_general(push, partner_float, scatter_dims, precision=lax.Precisio...]
    pallas_call x0 -> x3, Pallas kernels: none -> 84.8 us  [the longest x1 41 us: call_pairs(): pl.pallas_call(pairs_kernel, name='pairs', out_shape=(jax.ShapeDtypeStruc...]
    ppermute x6 -> x0, starting transfers between devices: 17.1 us -> none  [from_behind(): return lax.ppermute(value, axis, pairs)]
    ppermute x6 -> x0, waiting for transfers between devices: 16.2 us -> none  [from_behind(): return lax.ppermute(value, axis, pairs)]
    unnamed x40 -> x35, local copies, waits for them, and re-layouts: 0.67 us -> 11.8 us
  transfers between devices with their start and end apart: 6 -> 0, of which waited for: 5 -> 0; matrix products, arithmetic and copies ran while one was open for 41% -> 0% of each run, Pallas kernels for 0% -> 0%
where the time goes in v1:
time: 98 us; the launch traced here: 97.3 us
  Pallas kernels  84.8 us (87%)
  local copies, waits for them, and re-layouts  11.8 us (12%)
    pallas_call x1, Pallas kernels, call_pairs(): pl.pallas_call(pairs_kernel, name='pairs', out_shape=(jax.ShapeDtypeStruc...  41 us
    pallas_call x1, Pallas kernels, on_device(): pl.pallas_call(home_kernel, name='home', out_shape=(jax.ShapeDtypeStruct(...  24.7 us
    pallas_call x1, Pallas kernels, on_device(): pl.pallas_call(offer_kernel, name='offer', out_shape=(jax.ShapeDtypeStruc...  19.1 us
    unnamed x35, local copies, waits for them, and re-layouts  11.8 us

profile of v1, /device:TPU:1, one launch (start us, length us, event | category | flops | bytes accessed | tf_op | source)
XLA Modules:
  0.0 97.3 jit_solution(6845097803278495836)
XLA Ops:
  0.6 0.0 copy-start.14
  0.6 0.0 copy-start.2
  0.7 0.0 copy-start.3
  0.7 0.7 copy-done.14
  1.3 0.1 copy.19.radial_ref
  1.4 19.1 %offer.1 = (f32[8,512]{1,0:T(8,128)}, bf16[64,1024]{1,0:T(8,128)(2,1)}, bf16[7,80,256]{2,1,0:T(8,128)(2,1)}) custom-call(f32[3,512]{1,0:T(4,128)} %pos_ref.1, bf16[64,512]{1,0:T(8,128)(2,1)} %feat_ref.1, s32[1,512]{1,0:T(1,128)} %bitcast.20, bf16[1,4]{1,0:T(2,128)(2,1)} %bitcast.22, bf16[64,64]{1,0:T(8,128)(2,1)} %first_ref.1, bf16[64,64]{1,0:T(8,128)(2,1)} %second_ref.1, ...), custom_call_target="tpu_custom_call" | custom-call | tf_op jit(solution)/shard_map/offer/pallas_call | solution.py:319
  20.5 0.0 copy-start.13
  20.5 0.0 copy-done.2
  20.5 0.0 copy-done.3
  20.5 0.6 copy-done.13
  21.2 0.0 copy-start
  21.2 1.0 copy-done
  22.1 0.0 copy-start.1
  22.1 0.9 copy-done.1
  23.0 0.0 copy-start.4
  23.0 0.9 copy-done.4
  23.9 0.0 copy-start.6
  23.9 0.8 copy-done.6
  24.7 0.8 copy-done.7
  25.5 0.8 copy-done.8
  26.3 0.7 copy-done.9
  27.0 0.7 copy-done.10
  27.7 0.7 copy-done.11
  28.5 41.0 %pairs.1 = (f32[8,512]{1,0:T(8,128)S(1)}, f32[7,8,256]{2,1,0:T(8,128)S(1)}) custom-call(f32[8,512]{1,0:T(8,128)S(1)} %copy-done.11, bf16[64,1024]{1,0:T(8,128)(2,1)S(1)} %copy-done.1, bf16[7,80,256]{2,1,0:T(8,128)(2,1)S(1)} %copy-done, s32[160,128]{1,0:T(8,128)S(1)} %bitcast.11, s32[160,128]{1,0:T(8,128)S(1)} %bitcast.12, s32[160,128]{1,0:T(8,128)S(1)} %bitcast.13, ...), custom_call_target="tpu_custom_call" | custom-call | tf_op jit(solution)/shard_map/pairs/pallas_call | solution.py:295
  69.4 0.0 copy-start.5
  69.4 0.6 copy-done.5
  70.1 0.6 copy-done.12
  70.7 24.7 %home.1 = (f32[3,512]{1,0:T(4,128)}, f32[1,512]{1,0:T(1,128)}) custom-call(f32[8,512]{1,0:T(8,128)} %copy-done.12, f32[7,8,256]{2,1,0:T(8,128)} %copy-done.5, s32[1,256]{1,0:T(1,128)} %bitcast.19), custom_call_target="tpu_custom_call" | custom-call | tf_op jit(solution)/shard_map/home/pallas_call | solution.py:332
  95.4 0.0 copy-start.15
  95.4 1.3 %copy.22 = f32[3,512]{1,0:T(4,128)} copy(f32[3,512]{1,0:T(4,128)} %get-tuple-element.18) | data formatting | bytes 12288
  96.7 0.0 copy-done.15
  96.7 0.6 copy.23
  (6 shorter events, 0.0 us)
Async XLA Ops:
  0.6 0.7 copy-start.14
  0.6 19.9 %copy-start.2 = (s32[20480]{0:T(1024)S(1)}, s32[20480]{0:T(1024)}, u32[]{:S(2)}) copy-start(s32[20480]{0:T(1024)} %param.28) | copy-start | bytes 245764
  0.7 19.9 %copy-start.3 = (s32[20480]{0:T(1024)S(1)}, s32[20480]{0:T(1024)}, u32[]{:S(2)}) copy-start(s32[20480]{0:T(1024)} %param.29) | copy-start | bytes 245764
  20.5 0.7 copy-start.13
  21.2 1.0 copy-start
  22.1 0.9 copy-start.1
  23.0 0.9 copy-start.4
  23.9 0.8 copy-start.6
  24.7 0.8 copy-start.7
  25.5 0.8 copy-start.8
  26.3 0.7 copy-start.9
  27.0 0.7 copy-start.10
  27.7 0.7 copy-start.11
  69.4 0.6 copy-start.5
  70.1 0.6 copy-start.12
  95.4 1.3 %copy-start.15 = (f32[1,512]{1,0:T(1,128)S(1)}, f32[1,512]{1,0:T(1,128)}, u32[]{:S(2)}) copy-start(f32[1,512]{1,0:T(1,128)} %get-tuple-element.15) | copy-start | bytes 6148

commit v2 on v1

v2 whole, which is shorter than its diff:
```python
import jax
import jax.numpy as jnp
from jax import lax
from jax.experimental import pallas as pl
from jax.experimental.pallas import tpu as pltpu
from jax.sharding import PartitionSpec as P

OFFSETS = ((1, 0, 0), (0, 1, 0), (0, 0, 1), (1, 1, 0), (1, 0, 1), (0, 1, 1), (1, 1, 1))
DIRECT = (2, 0, 1, 3)
RELAYED = ((0, 4), (1, 5), (3, 6))
MESH_IDS = pl.DeviceIdType.MESH
ANY = pl.BlockSpec(memory_space=pl.ANY)
NT = (((1,), (1,)), ((), ()))
TN = (((0,), (0,)), ((), ()))
WIDTH = 24.0
F32, BF16, I32 = jnp.float32, jnp.bfloat16, jnp.int32
LIVE = 128
ROWS = 72
EARLY = 8
LATE = 4
HALVES = 4


def neighbour(offset, sign):
    where = []
    for axis, step in zip(("gx", "gy", "gz"), offset):
        count = lax.axis_size(axis)
        where.append(lax.rem(lax.axis_index(axis) + sign * step + count, count))
    return tuple(where)


def meet(offsets, sign):
    barrier = pltpu.get_barrier_semaphore()
    for offset in offsets:
        pl.semaphore_signal(barrier, inc=1, device_id=neighbour(offset, sign), device_id_type=MESH_IDS)
    return barrier


def move(sources, targets, sems):
    copies = [pltpu.make_async_copy(s, t, sems.at[k]) for k, (s, t) in enumerate(zip(sources, targets))]
    for copy in copies:
        copy.start()
    return copies


def finish(copies):
    for copy in copies:
        copy.wait()


def one_hot(row, count):
    levels = lax.broadcasted_iota(jnp.int16, (count, row.shape[1]), 0)
    return jnp.where(levels == row.astype(jnp.int16), jnp.ones((), BF16), jnp.zeros((), BF16))


def split_two(value):
    high = value.astype(BF16).astype(F32)
    return high, value - high


def take_lanes(table, index):
    return jnp.take_along_axis(table, index, axis=1, mode="promise_in_bounds")


def pick(tab, n, c, low, high):
    value = take_lanes(tab[c * n], low)
    for ch in range(1, n):
        value = jnp.where(high == ch, take_lanes(tab[c * n + ch], low), value)
    return value


def geometry(low_i, high_i, low_j, high_j, own_tab, tab, chunks, n):
    gap = [pick(tab, n, c, low_j, high_j) - pick(own_tab, chunks, c, low_i, high_i) for c in range(3)]
    return gap, gap[0] * gap[0] + gap[1] * gap[1] + gap[2] * gap[2]


def spread(row, tab, first):
    for ch in range(row.shape[1] // 128):
        tab[first + ch] = jnp.broadcast_to(row[:, 128 * ch:128 * ch + 128], (8, 128))


def compact(own_list, par_list, mask_list, own_tab, tab, chunks, n, words, live, ranks, packed):
    rows = own_list.shape[0]
    lane = lax.broadcasted_iota(I32, (8, 128), 1)

    def find(v, carry):
        at = pl.ds(pl.multiple_of(8 * v, 8), 8)
        own, partner = own_list[at, :], par_list[at, :]
        gap, squared = geometry(own & 127, own >> 7, partner & 127, partner >> 7, own_tab, tab, chunks, n)
        alive = jnp.logical_and(mask_list[at, :] > 0, squared < 1.0)
        live[at, :] = jnp.where(alive, 1.0, 0.0)
        words[at, :] = jnp.where(alive, (own << 8) + (partner << 17) + LIVE, 0)
        return carry
    lax.fori_loop(0, rows // 8, find, 0, unroll=4)
    above = jnp.where(lax.broadcasted_iota(I32, (128, 128), 0) < lax.broadcasted_iota(I32, (128, 128), 1), 1.0, 0.0)
    adder = jnp.concatenate([above, jnp.ones((128, 128), F32)], 1).astype(BF16)
    ranks[0:rows, :] = jnp.dot(live[0:rows, :].astype(BF16), adder, preferred_element_type=F32)

    tiles = rows // 8
    stand = jnp.zeros((8, 128), I32)
    slots = [jnp.zeros((8, 128), I32) for _ in range(tiles)]
    for v in range(tiles):
        at = slice(8 * v, 8 * v + 8)
        word = words[at, :]
        rank = ranks[at, 0:128].astype(I32)
        number = ranks[at, 128:256].astype(I32)
        word = jnp.where(word > 0, word + (lane - rank), 0)
        for bit in range(7):
            moved = pltpu.roll(word, 128 - (1 << bit), 1)
            stay = jnp.where((word & (1 << bit)) > 0, 0, word)
            word = jnp.where((moved & (1 << bit)) > 0, moved, stay)
        turn = (lane - stand) & 127
        word = take_lanes(word, turn)
        row = jnp.where(turn < number, (stand + turn) >> 7, -1)
        for t in range(v + 1):
            slots[t] = jnp.where(row == t, word, slots[t])
        stand = stand + number
    for t in range(tiles):
        packed[8 * t:8 * t + 8, :] = slots[t]
    return stand


def weights(radial, mid, last, out, w_mids, w_lasts, w_radials):
    nb, channels = radial.shape
    high, low = split_two(radial[...] * 0.5)
    spot = lax.broadcasted_iota(I32, (nb, 4 * nb), 1)
    term = lax.broadcasted_iota(I32, (nb, 4 * nb), 0)
    place_high = jnp.where((spot == term) | (spot == term + nb), 1.0, 0.0).astype(BF16)
    place_low = jnp.where(spot == term + 2 * nb, 1.0, 0.0).astype(BF16)
    w_radial = (lax.dot_general(high.astype(BF16), place_high, TN, preferred_element_type=F32)
                + lax.dot_general(low.astype(BF16), place_low, TN, preferred_element_type=F32)).astype(BF16)
    w_mid = (mid[...].astype(F32) * 0.5).astype(BF16)
    w_last = (last[...].astype(F32) * 0.5).astype(BF16)
    for store, w in ((w_mids, w_mid), (w_lasts, w_last), (w_radials, w_radial)):
        for half in range(HALVES):
            store[channels * half:channels * half + channels, :] = jnp.concatenate(
                [w if other == half else jnp.zeros_like(w) for other in range(HALVES)], 1)
    eye = lax.broadcasted_iota(I32, (channels, channels), 0) == lax.broadcasted_iota(I32, (channels, channels), 1)
    return jnp.sum(jnp.where(eye, jnp.broadcast_to(out[...], (channels, channels)), 0.0), 1, keepdims=True)


def activate(y, tangent):
    up = 1.0 + jnp.tanh(y)
    value = y * up
    return value, (up + value * (2.0 - up)) * tangent


def pair_step(packed, own_tab, tab, chunks, n, left_tab, right_tab, w_mids, w_lasts, w_radials, w_out,
              hot_own, hot_par, quant, acc_own, acc_par):
    nb = 8
    centers = lax.broadcasted_iota(I32, (nb, 128), 0).astype(F32) / (nb - 1)
    zero = jnp.zeros((), BF16)

    def step(t, carry):
        word = packed[pl.ds(pl.multiple_of(8 * t, 8), 8), :]
        own, partner = (word >> 8) & 511, word >> 17
        low_i, high_i, low_j, high_j = own & 127, own >> 7, partner & 127, partner >> 7
        wide = lambda x, half: jnp.concatenate([x[2 * half:2 * half + 1], x[2 * half + 1:2 * half + 2]], 1)

        def gather(low, high, keep, table, groups, half):
            hot = one_hot(wide(low, half), 128)
            keep[:, 256 * half:256 * half + 256] = hot
            top = wide(high, half)
            odd = jnp.broadcast_to((top & 1).astype(jnp.int16), (128, 256))
            hot = jnp.concatenate([jnp.where(odd == jnp.int16(0), hot, zero), jnp.where(odd == jnp.int16(1), hot, zero)], 0)
            found = jnp.dot(table[...], hot, preferred_element_type=F32)
            group = top >> 1
            value = found[0:64]
            for g in range(1, groups):
                value = jnp.where(group == g, found[64 * g:64 * g + 64], value)
            return value

        gathered = [gather(low_i, high_i, hot_own, left_tab, chunks // 2, half)
                    + gather(low_j, high_j, hot_par, right_tab, n // 2, half) for half in range(HALVES)]
        gap, squared = geometry(low_i, high_i, low_j, high_j, own_tab, tab, chunks, n)
        weight = jnp.where((word & LIVE) > 0, pick(own_tab, chunks, 3, low_i, high_i) * pick(tab, n, 3, low_j, high_j), 0.0)
        radials = []
        for half in range(HALVES):
            tiles, slants = [], []
            for r in (2 * half, 2 * half + 1):
                off = squared[r:r + 1] - centers
                basis = jnp.exp(-WIDTH * off * off)
                tiles.append(basis)
                slants.append((-2.0 * WIDTH) * off * basis)
            high, low = split_two(jnp.concatenate(tiles + slants, 1))
            radials += [high, low, high, jnp.zeros_like(low)]
        radials = jnp.dot(w_radials[...], jnp.concatenate(radials, 0).astype(BF16), preferred_element_type=F32)
        quarter = lambda x, half: x[64 * half:64 * half + 64]
        now = [activate(g + quarter(radials, half)[:, 0:256], quarter(radials, half)[:, 256:512]) for half, g in enumerate(gathered)]
        for w in (w_mids, w_lasts):
            stack = jnp.concatenate([jnp.concatenate(pair, 1).astype(BF16) for pair in now], 0)
            mixed = jnp.dot(w[...], stack, preferred_element_type=F32)
            now = [activate(quarter(mixed, half)[:, 0:256], quarter(mixed, half)[:, 256:512]) for half in range(HALVES)]
        reads = [jnp.sum(value * w_out, 0, keepdims=True) for value, _ in now]
        slopes = [jnp.sum(slope * w_out, 0, keepdims=True) for _, slope in now]
        tall = lambda xs: jnp.concatenate([x[:, 128 * k:128 * k + 128] for x in xs for k in range(2)], 0)
        readout, reslope = tall(reads), tall(slopes)
        near = jnp.maximum(1.0 - squared, 0.0)
        envelope = near * near
        energy = weight * envelope * readout
        slope = weight * (envelope * reslope - 2.0 * near * readout)
        outs = [2.0 * g * slope for g in gap] + [energy]
        for q, out in enumerate(outs):
            high, low = split_two(out)
            quant[8 * q:8 * q + 8, :] = high
            quant[32 + 8 * q:40 + 8 * q, :] = low
        a_own, a_par = [], []
        for r in range(8):
            tile = quant[pl.ds(r, 8, stride=8), :]
            a_own.append(jnp.concatenate([jnp.where(high_i[r:r + 1] == ch, tile, 0.0) for ch in range(chunks)], 0))
            a_par.append(jnp.concatenate([jnp.where(high_j[r:r + 1] == ch, tile, 0.0) for ch in range(n)], 0))
        acc_own[...] += lax.dot_general(jnp.concatenate(a_own, 1).astype(BF16), hot_own[...], NT, preferred_element_type=F32)
        acc_par[...] += lax.dot_general(jnp.concatenate(a_par, 1).astype(BF16), hot_par[...], NT, preferred_element_type=F32)
        return carry
    return step


def offer_kernel(pos_hbm, feat_hbm, species_hbm, scale_hbm, first_hbm, second_hbm, send_hbm,
                 one_hbm, two_hbm, mask_hbm, radial_hbm, mid_hbm, last_hbm, out_hbm,
                 own_out, left_out, right_out, ghost_out, packed_out, stand_out, acc_own_out, acc_loc_out,
                 pos, feat, species, scale, first, second, send, one, two, mask, radial, mid, last, out,
                 offered, own, left_tab, right_tab, packed, stand, acc_own, acc_loc,
                 own_tab, words, live, ranks, hot_own, hot_par, quant, w_mids, w_lasts, w_radials,
                 in_sem, out_sem, send_sem, recv_sem):
    paths = [OFFSETS[k] for k in DIRECT]
    barrier = meet(paths, 1)
    loads = move((pos_hbm, feat_hbm, species_hbm, scale_hbm, first_hbm, second_hbm, send_hbm,
                  one_hbm, two_hbm, mask_hbm, radial_hbm, mid_hbm, last_hbm, out_hbm),
                 (pos, feat, species, scale, first, second, send, one, two, mask, radial, mid, last, out), in_sem)
    finish(loads[0:7])
    count = pos.shape[1]
    chunks = count // 128
    where = pos[...]
    kinds = species[...]
    scales = scale[...].astype(F32)
    gain = jnp.zeros(kinds.shape, F32)
    for kind in range(scales.shape[1]):
        gain = jnp.where(kinds == kind, scales[:, kind:kind + 1], gain)
    right = (jnp.dot(second[...], feat[...], preferred_element_type=F32).astype(BF16).astype(F32) * 0.5).astype(BF16)
    high = where.astype(BF16).astype(F32)
    tail = jnp.concatenate([high, where - high, gain, jnp.zeros((9, count), F32)], 0).astype(BF16)
    payload = jnp.concatenate([right, tail], 0)
    offered[...] = jnp.dot(payload, one_hot(send[...], count), preferred_element_type=F32).astype(BF16)[0:ROWS]
    pl.semaphore_wait(barrier, len(paths))

    def remote(source, k, offset):
        copy = pltpu.make_async_remote_copy(
            src_ref=source, dst_ref=ghost_out.at[k], send_sem=send_sem.at[k], recv_sem=recv_sem.at[k],
            device_id=neighbour(offset, -1), device_id_type=MESH_IDS)
        copy.start()
        return copy
    copies = [remote(offered, k, OFFSETS[k]) for k in DIRECT]

    own[0:3, :] = where
    own[3:4, :] = gain
    own[4:8, :] = jnp.zeros((4, count), F32)
    left = (jnp.dot(first[...], feat[...], preferred_element_type=F32).astype(BF16).astype(F32) * 0.5).astype(BF16)
    for g in range(count // 256):
        left_tab[64 * g:64 * g + 64, :] = left[:, 256 * g:256 * g + 256]
        right_tab[64 * g:64 * g + 64, :] = right[:, 256 * g:256 * g + 256]
    for c in range(4):
        spread(own[c:c + 1, :], own_tab, c * chunks)
    finish(loads[7:])
    w_out = weights(radial, mid, last, out, w_mids, w_lasts, w_radials)
    copies[0].wait_recv()
    relays = [remote(ghost_out.at[2], k, OFFSETS[step]) for step, k in RELAYED]
    stand[...] = compact(one, two, mask, own_tab, own_tab, chunks, chunks, words, live, ranks, packed)
    acc_own[...] = jnp.zeros_like(acc_own)
    acc_loc[...] = jnp.zeros_like(acc_loc)
    step = pair_step(packed, own_tab, own_tab, chunks, chunks, left_tab, right_tab, w_mids, w_lasts, w_radials, w_out,
                     hot_own, hot_par, quant, acc_own, acc_loc)
    lax.fori_loop(0, EARLY, step, 0)
    stores = move((own, left_tab, right_tab, packed, stand, acc_own, acc_loc),
                  (own_out, left_out, right_out, packed_out, stand_out, acc_own_out, acc_loc_out), out_sem)
    copies[0].wait_send()
    finish(copies[1:])
    finish(relays)
    finish(stores)


def pairs_kernel(own_hbm, left_hbm, right_hbm, ghost_hbm, packed_hbm, stand_hbm, acc_own_hbm, acc_loc_hbm,
                 one_hbm, two_hbm, mask_hbm, radial_hbm, mid_hbm, last_hbm, out_hbm,
                 acc_own_out, acc_loc_out, force_out,
                 own, left_tab, right_tab, ghost, packed, stand, acc_own, acc_loc, one, two, mask, radial, mid, last, out,
                 own_tab, ghost_tab, gtable, gpacked, words, live, ranks, hot_own, hot_par, quant, acc_gho, force,
                 w_mids, w_lasts, w_radials, in_sem, out_sem):
    loads = move((own_hbm, ghost_hbm, one_hbm, two_hbm, mask_hbm, left_hbm, right_hbm, packed_hbm, stand_hbm,
                  acc_own_hbm, acc_loc_hbm, radial_hbm, mid_hbm, last_hbm, out_hbm),
                 (own, ghost, one, two, mask, left_tab, right_tab, packed, stand,
                  acc_own, acc_loc, radial, mid, last, out), in_sem)
    finish(loads)
    count = own.shape[1]
    chunks = count // 128
    sends = ghost.shape[2]
    per = sends // 128
    gchunks = len(OFFSETS) * per
    for c in range(4):
        spread(own[c:c + 1, :], own_tab, c * chunks)
    for k, offset in enumerate(OFFSETS):
        gtable[64 * k:64 * k + 64, :] = ghost[k, 0:64, :]
        tail = ghost[k, 64:72, :].astype(F32)
        for c in range(4):
            row = tail[c:c + 1] + tail[c + 3:c + 4] + float(offset[c]) if c < 3 else tail[6:7]
            spread(row, ghost_tab, c * gchunks + k * per)
    w_out = weights(radial, mid, last, out, w_mids, w_lasts, w_radials)
    gstand = compact(one, two, mask, own_tab, ghost_tab, chunks, gchunks, words, live, ranks, gpacked)
    acc_gho[...] = jnp.zeros_like(acc_gho)
    gstep = pair_step(gpacked, own_tab, ghost_tab, chunks, gchunks, left_tab, gtable, w_mids, w_lasts, w_radials, w_out,
                      hot_own, hot_par, quant, acc_own, acc_gho)
    lax.fori_loop(0, (jnp.max(gstand) + 127) >> 7, gstep, 0)
    for ch in range(gchunks):
        cols = slice(128 * (ch % per), 128 * (ch % per) + 128)
        force[ch // per, 0:4, cols] = acc_gho[8 * ch:8 * ch + 4, :] + acc_gho[8 * ch + 4:8 * ch + 8, :]
        force[ch // per, 4:8, cols] = jnp.zeros((4, 128), F32)
    step = pair_step(packed, own_tab, own_tab, chunks, chunks, left_tab, right_tab, w_mids, w_lasts, w_radials, w_out,
                     hot_own, hot_par, quant, acc_own, acc_loc)
    lax.fori_loop(EARLY + LATE, (jnp.max(stand[...]) + 127) >> 7, step, 0)
    finish(move((acc_own, acc_loc, force), (acc_own_out, acc_loc_out, force_out), out_sem))


def home_kernel(own_hbm, left_hbm, right_hbm, packed_hbm, acc_own_hbm, acc_loc_hbm, force_hbm, send_hbm,
                radial_hbm, mid_hbm, last_hbm, out_hbm,
                force_out, energy_out,
                own, left_tab, right_tab, packed, acc_own, acc_loc, force, send, radial, mid, last, out,
                arrived, own_tab, hot_own, hot_par, quant, w_mids, w_lasts, w_radials, result, energy,
                in_sem, out_sem, send_sem, recv_sem):
    barrier = meet(OFFSETS, -1)
    loads = move((force_hbm, own_hbm, left_hbm, right_hbm, packed_hbm, acc_own_hbm, acc_loc_hbm, send_hbm,
                  radial_hbm, mid_hbm, last_hbm, out_hbm),
                 (force, own, left_tab, right_tab, packed, acc_own, acc_loc, send, radial, mid, last, out), in_sem)
    loads[0].wait()
    pl.semaphore_wait(barrier, len(OFFSETS))
    copies = []
    for k, offset in enumerate(OFFSETS):
        copy = pltpu.make_async_remote_copy(
            src_ref=force.at[k], dst_ref=arrived.at[k], send_sem=send_sem.at[k], recv_sem=recv_sem.at[k],
            device_id=neighbour(offset, 1), device_id_type=MESH_IDS)
        copy.start()
        copies.append(copy)
    finish(loads[1:])
    count = own.shape[1]
    chunks = count // 128
    for c in range(4):
        spread(own[c:c + 1, :], own_tab, c * chunks)
    w_out = weights(radial, mid, last, out, w_mids, w_lasts, w_radials)
    step = pair_step(packed, own_tab, own_tab, chunks, chunks, left_tab, right_tab, w_mids, w_lasts, w_radials, w_out,
                     hot_own, hot_par, quant, acc_own, acc_loc)
    lax.fori_loop(EARLY, EARLY + LATE, step, 0)
    hot = one_hot(send[...], count)
    finish(copies)
    total = arrived[0]
    for k in range(1, len(OFFSETS)):
        total = total + arrived[k]
    high, rest = split_two(total)
    mid_part, low = split_two(rest)
    parts = jnp.concatenate([high, mid_part, low, jnp.zeros_like(low)], 0).astype(BF16)
    back = lax.dot_general(parts, hot, NT, preferred_element_type=F32)
    back = back[0:8] + back[8:16] + back[16:24]
    for ch in range(chunks):
        cols = slice(128 * ch, 128 * ch + 128)
        mine = acc_own[8 * ch:8 * ch + 4, :] + acc_own[8 * ch + 4:8 * ch + 8, :]
        other = acc_loc[8 * ch:8 * ch + 4, :] + acc_loc[8 * ch + 4:8 * ch + 8, :]
        result[:, cols] = mine[0:3] - other[0:3] - back[0:3, cols]
        energy[:, cols] = mine[3:4]
    finish(move((result, energy), (force_out, energy_out), out_sem))


def on_device(positions, features, species, species_scale, w_first, w_second, w_radial, w_mid, w_last, w_out,
              ghost_send, local_first, local_second, local_mask, ghost_owner, ghost_index, ghost_mask):
    v, shape = pltpu.VMEM, jax.ShapeDtypeStruct
    count = positions.shape[1]
    sends = ghost_send.shape[0]
    channels, nb = w_radial.shape
    blocks = len(OFFSETS)
    chunks, gchunks = count // 128, blocks * sends // 128
    lrows, grows = local_first.shape[0] // 128, ghost_owner.shape[0] // 128
    buffers = lambda arrays: [v(x.shape, x.dtype) for x in arrays]
    sems = lambda number: pltpu.SemaphoreType.DMA((number,))
    send_row = ghost_send.reshape(1, sends)
    net = [w_radial.T, w_mid, w_last, w_out.reshape(1, channels)]
    local = [x.reshape(lrows, 128) for x in (local_first, local_second, local_mask)]
    ghostly = [x.reshape(grows, 128) for x in (ghost_owner, ghost_index, ghost_mask)]
    blocks_w = [v((4 * channels, 4 * channels), BF16), v((4 * channels, 4 * channels), BF16), v((4 * channels, 16 * nb), BF16)]
    hots = [v((128, 1024), BF16), v((128, 1024), BF16), v((64, 128), F32)]
    table = shape((channels * count // 256, 256), BF16)
    acc = shape((8 * chunks, 128), F32)
    own_tab = v((4 * chunks, 8, 128), F32)

    args = [positions, features, species.reshape(1, count), species_scale.reshape(1, -1), w_first, w_second, send_row] + local + net
    made = [shape((8, count), F32), table, table, shape((blocks, ROWS, sends), BF16),
            shape((lrows, 128), I32), shape((8, 128), I32), acc, acc]
    own, left_tab, right_tab, ghosts, packed, stand, acc_own, acc_loc = pl.pallas_call(
        offer_kernel,
        name="offer",
        out_shape=made,
        in_specs=[ANY] * len(args),
        out_specs=[ANY] * len(made),
        scratch_shapes=buffers(args) + [v((ROWS, sends), BF16)] + buffers(made[0:3] + made[4:]) + [
            own_tab, v((lrows, 128), I32), v((lrows, 128), F32), v((lrows, 256), F32)] + hots + blocks_w + [
            sems(len(args)), sems(len(made) - 1), sems(blocks), sems(blocks)],
        compiler_params=pltpu.CompilerParams(collective_id=0, has_side_effects=True, vmem_limit_bytes=48 << 20),
    )(*args)

    args = [own, left_tab, right_tab, ghosts, packed, stand, acc_own, acc_loc] + ghostly + net
    made = [acc, acc, shape((blocks, 8, sends), F32)]
    acc_own, acc_loc, gforce = pl.pallas_call(
        pairs_kernel,
        name="pairs",
        out_shape=made,
        in_specs=[ANY] * len(args),
        out_specs=[ANY] * len(made),
        scratch_shapes=buffers(args) + [
            own_tab, v((4 * gchunks, 8, 128), F32), v((channels * gchunks // 2, 256), BF16), v((grows, 128), I32),
            v((grows, 128), I32), v((grows, 128), F32), v((grows, 256), F32)] + hots + [
            v((8 * gchunks, 128), F32), v((blocks, 8, sends), F32)] + blocks_w + [sems(len(args)), sems(len(made))],
        compiler_params=pltpu.CompilerParams(vmem_limit_bytes=48 << 20),
    )(*args)

    args = [own, left_tab, right_tab, packed, acc_own, acc_loc, gforce, send_row] + net
    made = [shape((3, count), F32), shape((1, count), F32)]
    forces, energy = pl.pallas_call(
        home_kernel,
        name="home",
        out_shape=made,
        in_specs=[ANY] * len(args),
        out_specs=[ANY] * len(made),
        scratch_shapes=buffers(args) + [v((blocks, 8, sends), F32), own_tab] + hots + blocks_w + buffers(made) + [
            sems(len(args)), sems(len(made)), sems(blocks), sems(blocks)],
        compiler_params=pltpu.CompilerParams(collective_id=1, has_side_effects=True, vmem_limit_bytes=48 << 20),
    )(*args)
    return forces, energy.reshape(count)


def solution(mesh):
    everywhere = ("gx", "gy", "gz")
    wide, flat, copied = P(None, everywhere), P(everywhere), P()
    in_specs = (wide, wide, flat) + (copied,) * 7 + (flat,) * 7
    return jax.shard_map(on_device, mesh=mesh, in_specs=in_specs, out_specs=(wide, flat), check_vma=False)
```

time: 98 us -> 58.3 us (0.59)
  Pallas kernels: 84.8 us -> 46.8 us
  local copies, waits for them, and re-layouts: 11.8 us -> 10.2 us
    pallas_call x3, Pallas kernels: 84.8 us -> 46.8 us  [the longest x1 22.6 us: on_device(): pl.pallas_call(offer_kernel, name='offer', out_shape=made, in_specs=[ANY]...]
    unnamed x35 -> x36, local copies, waits for them, and re-layouts: 11.8 us -> 10.2 us
where the time goes in v2:
time: 58.3 us; the launch traced here: 57.7 us
  Pallas kernels  46.8 us (80%)
  local copies, waits for them, and re-layouts  10.2 us (17%)
  between operations  0.72 us (1%)
    pallas_call x1, Pallas kernels, on_device(): pl.pallas_call(offer_kernel, name='offer', out_shape=made, in_specs=[ANY]...  22.6 us
    pallas_call x1, Pallas kernels, on_device(): pl.pallas_call(home_kernel, name='home', out_shape=made, in_specs=[ANY] *...  16.7 us
    unnamed x36, local copies, waits for them, and re-layouts  10.2 us
    pallas_call x1, Pallas kernels, on_device(): pl.pallas_call(pairs_kernel, name='pairs', out_shape=made, in_specs=[ANY]...  7.45 us

profile of v2, /device:TPU:1, one launch (start us, length us, event | category | flops | bytes accessed | tf_op | source)
XLA Modules:
  0.0 57.7 jit_solution(484205093576435290)
XLA Ops:
  0.6 0.0 copy-start
  0.6 0.0 copy-start.9
  0.7 0.0 copy-start.13
  0.7 0.7 %copy-done = bf16[64,64]{1,0:T(8,128)(2,1)S(1)} copy-done((bf16[64,64]{1,0:T(8,128)(2,1)S(1)}, bf16[64,64]{1,0:T(8,128)(2,1)}, u32[]{:S(2)}) %copy-start) | copy-done | bytes 8216
  1.4 0.0 copy-done.9
  1.4 0.0 copy-done.13
  1.4 0.0 copy-start.1
  1.4 0.7 %copy-done.1 = bf16[64,64]{1,0:T(8,128)(2,1)S(1)} copy-done((bf16[64,64]{1,0:T(8,128)(2,1)S(1)}, bf16[64,64]{1,0:T(8,128)(2,1)}, u32[]{:S(2)}) %copy-start.1) | copy-done | bytes 8216
  2.1 0.0 copy-start.2
  2.1 0.9 %copy-done.2 = s32[20480]{0:T(1024)S(1)} copy-done((s32[20480]{0:T(1024)S(1)}, s32[20480]{0:T(1024)}, u32[]{:S(2)}) %copy-start.2) | copy-done | bytes 81944
  3.0 0.0 copy-start.3
  3.0 0.9 %copy-done.3 = s32[20480]{0:T(1024)S(1)} copy-done((s32[20480]{0:T(1024)S(1)}, s32[20480]{0:T(1024)}, u32[]{:S(2)}) %copy-start.3) | copy-done | bytes 81944
  3.9 0.0 copy-start.4
  3.9 0.9 %copy-done.4 = s32[20480]{0:T(1024)S(1)} copy-done((s32[20480]{0:T(1024)S(1)}, s32[20480]{0:T(1024)}, u32[]{:S(2)}) %copy-start.4) | copy-done | bytes 81944
  4.7 0.0 copy-start.5
  4.7 0.8 %copy-done.5 = bf16[64,512]{1,0:T(8,128)(2,1)S(1)} copy-done((bf16[64,512]{1,0:T(8,128)(2,1)S(1)}, bf16[64,512]{1,0:T(8,128)(2,1)}, u32[]{:S(2)}) %copy-start.5) | copy-done | bytes 65560
  5.6 0.0 copy-start.10
  5.6 0.7 %copy-done.10 = bf16[64,64]{1,0:T(8,128)(2,1)S(1)} copy-done((bf16[64,64]{1,0:T(8,128)(2,1)S(1)}, bf16[64,64]{1,0:T(8,128)(2,1)}, u32[]{:S(2)}) %copy-start.10) | copy-done | bytes 8216
  6.3 0.0 copy-start.11
  6.3 0.7 %copy-done.11 = bf16[64,64]{1,0:T(8,128)(2,1)S(1)} copy-done((bf16[64,64]{1,0:T(8,128)(2,1)S(1)}, bf16[64,64]{1,0:T(8,128)(2,1)}, u32[]{:S(2)}) %copy-start.11) | copy-done | bytes 8216
  7.0 0.7 %copy-done.12 = f32[3,512]{1,0:T(4,128)S(1)} copy-done((f32[3,512]{1,0:T(4,128)S(1)}, f32[3,512]{1,0:T(4,128)}, u32[]{:S(2)}) %copy-start.12) | copy-done | bytes 6168
  7.7 0.7 %copy-done.14 = s32[256]{0:T(256)S(1)} copy-done((s32[256]{0:T(256)S(1)}, s32[256]{0:T(256)}, u32[]{:S(2)}) %copy-start.14) | copy-done | bytes 1048
  8.4 0.7 %copy-done.15 = s32[512]{0:T(512)S(1)} copy-done((s32[512]{0:T(512)S(1)}, s32[512]{0:T(512)}, u32[]{:S(2)}) %copy-start.15) | copy-done | bytes 2072
  9.1 0.7 %copy-done.16 = bf16[4]{0:T(256)(128)(2,1)S(1)} copy-done((bf16[4]{0:T(256)(128)(2,1)S(1)}, bf16[4]{0:T(256)(128)(2,1)}, u32[]{:S(2)}) %copy-start.16) | copy-done | bytes 32
  9.7 22.6 %offer.1 = (f32[8,512]{1,0:T(8,128)S(1)}, bf16[128,256]{1,0:T(8,128)(2,1)S(1)}, bf16[128,256]{1,0:T(8,128)(2,1)S(1)}, bf16[7,72,256]{2,1,0:T(8,128)(2,1)S(1)}, s...) custom-call(f32[3,512]{1,0:T(4,128)S(1)} %copy-done.12, ...), custom_call_target="tpu_custom_call" | custom-call | tf_op jit(solution)/shard_map/offer/pallas_call | solution.py:392
  32.4 0.0 copy-done.6
  32.4 0.0 copy-done.7
  32.4 0.0 copy-done.8
  32.4 7.5 %pairs.1 = (f32[32,128]{1,0:T(8,128)S(1)}, f32[32,128]{1,0:T(8,128)S(1)}, f32[7,8,256]{2,1,0:T(8,128)S(1)}) custom-call(f32[8,512]{1,0:T(8,128)S(1)} %get-tuple-element.15.own_hbm, bf16[128,256]{1,0:T(8,128)(2,1)S(1)} %get-tuple-element.16.left_hbm, bf16[128,256]{1,0:T(8,128)(2,1)S(1)} %get-tuple-element.17.right_hbm, ...), custom_call_target="tpu_custom_call" | custom-call | tf_op jit(solution)/shard_map/pairs/pallas_call | solution.py:406
  39.9 16.7 %home.1 = (f32[3,512]{1,0:T(4,128)S(1)}, f32[1,512]{1,0:T(1,128)S(1)}) custom-call(f32[8,512]{1,0:T(8,128)S(1)} %get-tuple-element.15.own_hbm, bf16[128,256]{1,0:T(8,128)(2,1)S(1)} %get-tuple-element.16.left_hbm, bf16[128,256]{1,0:T(8,128)(2,1)S(1)} %get-tuple-element.17.right_hbm, s32[160,128]{1,0:T(8,128)S(1)} %get-tuple-element.18.packed_hbm, ...), custom_call_target="tpu_custom_call" | custom-call | tf_op jit(solution)/shard_map/home/pallas_call | solution.py:421
  56.6 0.6 %copy.21 = f32[3,512]{1,0:T(4,128)} copy(f32[3,512]{1,0:T(4,128)S(1)} %get-tuple-element.30) | data formatting | bytes 12288
  57.2 0.6 %copy.22 = f32[512]{0:T(512)} copy(f32[512]{0:T(512)S(1)} %bitcast.27) | data formatting | bytes 4096
  (7 shorter events, 0.0 us)
Async XLA Ops:
  0.6 0.7 %copy-start = (bf16[64,64]{1,0:T(8,128)(2,1)S(1)}, bf16[64,64]{1,0:T(8,128)(2,1)}, u32[]{:S(2)}) copy-start(bf16[64,64]{1,0:T(8,128)(2,1)} %mid_hbm.5) | copy-start | bytes 24580
  0.6 0.7 %copy-start.9 = (f32[64,8]{0,1:T(8,128)S(1)}, f32[64,8]{0,1:T(8,128)}, u32[]{:S(2)}) copy-start(f32[64,8]{0,1:T(8,128)} %param.23) | copy-start | bytes 6148
  0.7 0.7 %copy-start.13 = (f32[64]{0:T(128)S(1)}, f32[64]{0:T(128)}, u32[]{:S(2)}) copy-start(f32[64]{0:T(128)} %param.26) | copy-start | bytes 772
  1.4 0.7 %copy-start.1 = (bf16[64,64]{1,0:T(8,128)(2,1)S(1)}, bf16[64,64]{1,0:T(8,128)(2,1)}, u32[]{:S(2)}) copy-start(bf16[64,64]{1,0:T(8,128)(2,1)} %last_hbm.5) | copy-start | bytes 24580
  2.1 0.9 %copy-start.2 = (s32[20480]{0:T(1024)S(1)}, s32[20480]{0:T(1024)}, u32[]{:S(2)}) copy-start(s32[20480]{0:T(1024)} %param.28) | copy-start | bytes 245764
  3.0 0.9 %copy-start.3 = (s32[20480]{0:T(1024)S(1)}, s32[20480]{0:T(1024)}, u32[]{:S(2)}) copy-start(s32[20480]{0:T(1024)} %param.29) | copy-start | bytes 245764
  3.9 0.9 %copy-start.4 = (s32[20480]{0:T(1024)S(1)}, s32[20480]{0:T(1024)}, u32[]{:S(2)}) copy-start(s32[20480]{0:T(1024)} %param.30) | copy-start | bytes 245764
  4.7 0.8 %copy-start.5 = (bf16[64,512]{1,0:T(8,128)(2,1)S(1)}, bf16[64,512]{1,0:T(8,128)(2,1)}, u32[]{:S(2)}) copy-start(bf16[64,512]{1,0:T(8,128)(2,1)} %feat_hbm.1) | copy-start | bytes 196612
  5.6 0.7 %copy-start.10 = (bf16[64,64]{1,0:T(8,128)(2,1)S(1)}, bf16[64,64]{1,0:T(8,128)(2,1)}, u32[]{:S(2)}) copy-start(bf16[64,64]{1,0:T(8,128)(2,1)} %first_hbm.1) | copy-start | bytes 24580
  6.3 0.7 %copy-start.11 = (bf16[64,64]{1,0:T(8,128)(2,1)S(1)}, bf16[64,64]{1,0:T(8,128)(2,1)}, u32[]{:S(2)}) copy-start(bf16[64,64]{1,0:T(8,128)(2,1)} %second_hbm.1) | copy-start | bytes 24580
  7.0 0.7 %copy-start.12 = (f32[3,512]{1,0:T(4,128)S(1)}, f32[3,512]{1,0:T(4,128)}, u32[]{:S(2)}) copy-start(f32[3,512]{1,0:T(4,128)} %pos_hbm.1) | copy-start | bytes 18436
  7.7 0.7 %copy-start.14 = (s32[256]{0:T(256)S(1)}, s32[256]{0:T(256)}, u32[]{:S(2)}) copy-start(s32[256]{0:T(256)} %param.27) | copy-start | bytes 3076
  8.4 0.7 %copy-start.15 = (s32[512]{0:T(512)S(1)}, s32[512]{0:T(512)}, u32[]{:S(2)}) copy-start(s32[512]{0:T(512)} %param.19) | copy-start | bytes 6148
  9.1 0.7 %copy-start.16 = (bf16[4]{0:T(256)(128)(2,1)S(1)}, bf16[4]{0:T(256)(128)(2,1)}, u32[]{:S(2)}) copy-start(bf16[4]{0:T(256)(128)(2,1)} %param.20) | copy-start | bytes 28
  9.7 22.7 %copy-start.6 = (s32[12288]{0:T(1024)S(1)}, s32[12288]{0:T(1024)}, u32[]{:S(2)}) copy-start(s32[12288]{0:T(1024)} %param.31) | copy-start | bytes 147460
  9.7 22.7 %copy-start.7 = (s32[12288]{0:T(1024)S(1)}, s32[12288]{0:T(1024)}, u32[]{:S(2)}) copy-start(s32[12288]{0:T(1024)} %param.32) | copy-start | bytes 147460
  9.7 22.7 %copy-start.8 = (s32[12288]{0:T(1024)S(1)}, s32[12288]{0:T(1024)}, u32[]{:S(2)}) copy-start(s32[12288]{0:T(1024)} %param.33) | copy-start | bytes 147460

commit v3 on v2

--- a/solution.py
+++ b/solution.py
@@ -9,7 +9,7 @@
 DIRECT = (2, 0, 1, 3)
 RELAYED = ((0, 4), (1, 5), (3, 6))
 MESH_IDS = pl.DeviceIdType.MESH
-ANY = pl.BlockSpec(memory_space=pl.ANY)
+HBM = pl.BlockSpec(memory_space=pltpu.HBM)
 NT = (((1,), (1,)), ((), ()))
 TN = (((0,), (0,)), ((), ()))
 WIDTH = 24.0
@@ -19,6 +19,8 @@
 EARLY = 8
 LATE = 4
 HALVES = 4
+U = 2
+LAG = 0
 
 
 def neighbour(offset, sign):
@@ -151,7 +153,7 @@
     centers = lax.broadcasted_iota(I32, (nb, 128), 0).astype(F32) / (nb - 1)
     zero = jnp.zeros((), BF16)
 
-    def step(t, carry):
+    def stages(t, u):
         word = packed[pl.ds(pl.multiple_of(8 * t, 8), 8), :]
         own, partner = (word >> 8) & 511, word >> 17
         low_i, high_i, low_j, high_j = own & 127, own >> 7, partner & 127, partner >> 7
@@ -159,7 +161,7 @@
 
         def gather(low, high, keep, table, groups, half):
             hot = one_hot(wide(low, half), 128)
-            keep[:, 256 * half:256 * half + 256] = hot
+            keep[u, :, 256 * half:256 * half + 256] = hot
             top = wide(high, half)
             odd = jnp.broadcast_to((top & 1).astype(jnp.int16), (128, 256))
             hot = jnp.concatenate([jnp.where(odd == jnp.int16(0), hot, zero), jnp.where(odd == jnp.int16(1), hot, zero)], 0)
@@ -172,6 +174,7 @@
 
         gathered = [gather(low_i, high_i, hot_own, left_tab, chunks // 2, half)
                     + gather(low_j, high_j, hot_par, right_tab, n // 2, half) for half in range(HALVES)]
+        yield
         gap, squared = geometry(low_i, high_i, low_j, high_j, own_tab, tab, chunks, n)
         weight = jnp.where((word & LIVE) > 0, pick(own_tab, chunks, 3, low_i, high_i) * pick(tab, n, 3, low_j, high_j), 0.0)
         radials = []
@@ -185,14 +188,17 @@
             high, low = split_two(jnp.concatenate(tiles + slants, 1))
             radials += [high, low, high, jnp.zeros_like(low)]
         radials = jnp.dot(w_radials[...], jnp.concatenate(radials, 0).astype(BF16), preferred_element_type=F32)
+        yield
         quarter = lambda x, half: x[64 * half:64 * half + 64]
         now = [activate(g + quarter(radials, half)[:, 0:256], quarter(radials, half)[:, 256:512]) for half, g in enumerate(gathered)]
         for w in (w_mids, w_lasts):
             stack = jnp.concatenate([jnp.concatenate(pair, 1).astype(BF16) for pair in now], 0)
             mixed = jnp.dot(w[...], stack, preferred_element_type=F32)
+            yield
             now = [activate(quarter(mixed, half)[:, 0:256], quarter(mixed, half)[:, 256:512]) for half in range(HALVES)]
         reads = [jnp.sum(value * w_out, 0, keepdims=True) for value, _ in now]
         slopes = [jnp.sum(slope * w_out, 0, keepdims=True) for _, slope in now]
+        yield
         tall = lambda xs: jnp.concatenate([x[:, 128 * k:128 * k + 128] for x in xs for k in range(2)], 0)
         readout, reslope = tall(reads), tall(slopes)
         near = jnp.maximum(1.0 - squared, 0.0)
@@ -202,17 +208,34 @@
         outs = [2.0 * g * slope for g in gap] + [energy]
         for q, out in enumerate(outs):
             high, low = split_two(out)
-            quant[8 * q:8 * q + 8, :] = high
-            quant[32 + 8 * q:40 + 8 * q, :] = low
+            quant[u, 8 * q:8 * q + 8, :] = high
+            quant[u, 32 + 8 * q:40 + 8 * q, :] = low
         a_own, a_par = [], []
         for r in range(8):
-            tile = quant[pl.ds(r, 8, stride=8), :]
+            tile = quant[u, pl.ds(r, 8, stride=8), :]
             a_own.append(jnp.concatenate([jnp.where(high_i[r:r + 1] == ch, tile, 0.0) for ch in range(chunks)], 0))
             a_par.append(jnp.concatenate([jnp.where(high_j[r:r + 1] == ch, tile, 0.0) for ch in range(n)], 0))
-        acc_own[...] += lax.dot_general(jnp.concatenate(a_own, 1).astype(BF16), hot_own[...], NT, preferred_element_type=F32)
-        acc_par[...] += lax.dot_general(jnp.concatenate(a_par, 1).astype(BF16), hot_par[...], NT, preferred_element_type=F32)
+        acc_own[...] += lax.dot_general(jnp.concatenate(a_own, 1).astype(BF16), hot_own[u], NT, preferred_element_type=F32)
+        acc_par[...] += lax.dot_general(jnp.concatenate(a_par, 1).astype(BF16), hot_par[u], NT, preferred_element_type=F32)
+
+    def step(t, carry):
+        streams = [stages(U * t + u, u) for u in range(U)]
+        done, clock = 0, 0
+        while done < U:
+            for u, stream in enumerate(streams):
+                if stream is not None and clock >= LAG * u:
+                    try:
+                        next(stream)
+                    except StopIteration:
+                        streams[u] = None
+                        done += 1
+            clock += 1
         return carry
     return step
+
+
+def trips(stand):
+    return (jnp.max(stand) + 128 * U - 1) // (128 * U)
 
 
 def offer_kernel(pos_hbm, feat_hbm, species_hbm, scale_hbm, first_hbm, second_hbm, send_hbm,
@@ -269,7 +292,7 @@
     acc_loc[...] = jnp.zeros_like(acc_loc)
     step = pair_step(packed, own_tab, own_tab, chunks, chunks, left_tab, right_tab, w_mids, w_lasts, w_radials, w_out,
                      hot_own, hot_par, quant, acc_own, acc_loc)
-    lax.fori_loop(0, EARLY, step, 0)
+    lax.fori_loop(0, EARLY // U, step, 0)
     stores = move((own, left_tab, right_tab, packed, stand, acc_own, acc_loc),
                   (own_out, left_out, right_out, packed_out, stand_out, acc_own_out, acc_loc_out), out_sem)
     copies[0].wait_send()
@@ -307,14 +330,14 @@
     acc_gho[...] = jnp.zeros_like(acc_gho)
     gstep = pair_step(gpacked, own_tab, ghost_tab, chunks, gchunks, left_tab, gtable, w_mids, w_lasts, w_radials, w_out,
                       hot_own, hot_par, quant, acc_own, acc_gho)
-    lax.fori_loop(0, (jnp.max(gstand) + 127) >> 7, gstep, 0)
+    lax.fori_loop(0, trips(gstand), gstep, 0)
     for ch in range(gchunks):
         cols = slice(128 * (ch % per), 128 * (ch % per) + 128)
         force[ch // per, 0:4, cols] = acc_gho[8 * ch:8 * ch + 4, :] + acc_gho[8 * ch + 4:8 * ch + 8, :]
         force[ch // per, 4:8, cols] = jnp.zeros((4, 128), F32)
     step = pair_step(packed, own_tab, own_tab, chunks, chunks, left_tab, right_tab, w_mids, w_lasts, w_radials, w_out,
                      hot_own, hot_par, quant, acc_own, acc_loc)
-    lax.fori_loop(EARLY + LATE, (jnp.max(stand[...]) + 127) >> 7, step, 0)
+    lax.fori_loop((EARLY + LATE) // U, trips(stand[...]), step, 0)
     finish(move((acc_own, acc_loc, force), (acc_own_out, acc_loc_out, force_out), out_sem))
 
 
@@ -345,7 +368,7 @@
     w_out = weights(radial, mid, last, out, w_mids, w_lasts, w_radials)
     step = pair_step(packed, own_tab, own_tab, chunks, chunks, left_tab, right_tab, w_mids, w_lasts, w_radials, w_out,
                      hot_own, hot_par, quant, acc_own, acc_loc)
-    lax.fori_loop(EARLY, EARLY + LATE, step, 0)
+    lax.fori_loop(EARLY // U, (EARLY + LATE) // U, step, 0)
     hot = one_hot(send[...], count)
     finish(copies)
     total = arrived[0]
@@ -381,7 +404,7 @@
     local = [x.reshape(lrows, 128) for x in (local_first, local_second, local_mask)]
     ghostly = [x.reshape(grows, 128) for x in (ghost_owner, ghost_index, ghost_mask)]
     blocks_w = [v((4 * channels, 4 * channels), BF16), v((4 * channels, 4 * channels), BF16), v((4 * channels, 16 * nb), BF16)]
-    hots = [v((128, 1024), BF16), v((128, 1024), BF16), v((64, 128), F32)]
+    hots = [v((U, 128, 1024), BF16), v((U, 128, 1024), BF16), v((U, 64, 128), F32)]
     table = shape((channels * count // 256, 256), BF16)
     acc = shape((8 * chunks, 128), F32)
     own_tab = v((4 * chunks, 8, 128), F32)
@@ -393,12 +416,12 @@
         offer_kernel,
         name="offer",
         out_shape=made,
-        in_specs=[ANY] * len(args),
-        out_specs=[ANY] * len(made),
+        in_specs=[HBM] * len(args),
+        out_specs=[HBM] * len(made),
         scratch_shapes=buffers(args) + [v((ROWS, sends), BF16)] + buffers(made[0:3] + made[4:]) + [
             own_tab, v((lrows, 128), I32), v((lrows, 128), F32), v((lrows, 256), F32)] + hots + blocks_w + [
             sems(len(args)), sems(len(made) - 1), sems(blocks), sems(blocks)],
-        compiler_params=pltpu.CompilerParams(collective_id=0, has_side_effects=True, vmem_limit_bytes=48 << 20),
+        compiler_params=pltpu.CompilerParams(collective_id=0, has_side_effects=True, vmem_limit_bytes=60 << 20),
     )(*args)
 
     args = [own, left_tab, right_tab, ghosts, packed, stand, acc_own, acc_loc] + ghostly + net
@@ -407,13 +430,13 @@
         pairs_kernel,
         name="pairs",
         out_shape=made,
-        in_specs=[ANY] * len(args),
-        out_specs=[ANY] * len(made),
+        in_specs=[HBM] * len(args),
+        out_specs=[HBM] * len(made),
         scratch_shapes=buffers(args) + [
             own_tab, v((4 * gchunks, 8, 128), F32), v((channels * gchunks // 2, 256), BF16), v((grows, 128), I32),
             v((grows, 128), I32), v((grows, 128), F32), v((grows, 256), F32)] + hots + [
             v((8 * gchunks, 128), F32), v((blocks, 8, sends), F32)] + blocks_w + [sems(len(args)), sems(len(made))],
-        compiler_params=pltpu.CompilerParams(vmem_limit_bytes=48 << 20),
+        compiler_params=pltpu.CompilerParams(vmem_limit_bytes=60 << 20),
     )(*args)
 
     args = [own, left_tab, right_tab, packed, acc_own, acc_loc, gforce, send_row] + net
@@ -422,11 +445,11 @@
         home_kernel,
         name="home",
         out_shape=made,
-        in_specs=[ANY] * len(args),
-        out_specs=[ANY] * len(made),
+        in_specs=[HBM] * len(args),
+        out_specs=[HBM] * len(made),
         scratch_shapes=buffers(args) + [v((blocks, 8, sends), F32), own_tab] + hots + blocks_w + buffers(made) + [
             sems(len(args)), sems(len(made)), sems(blocks), sems(blocks)],
-        compiler_params=pltpu.CompilerParams(collective_id=1, has_side_effects=True, vmem_limit_bytes=48 << 20),
+        compiler_params=pltpu.CompilerParams(collective_id=1, has_side_effects=True, vmem_limit_bytes=60 << 20),
     )(*args)
     return forces, energy.reshape(count)
 

time: 58.3 us -> 48.2 us (0.83)
  local copies, waits for them, and re-layouts: 10.2 us -> 1.88 us
  Pallas kernels: 46.8 us -> 45.4 us
    unnamed x36 -> x4, local copies, waits for them, and re-layouts: 10.2 us -> 1.88 us
    pallas_call x3, Pallas kernels: 46.8 us -> 45.4 us  [the longest x1 20.3 us: on_device(): pl.pallas_call(offer_kernel, name='offer', out_shape=made, in_specs=[HBM]...]
where the time goes in v3:
time: 48.2 us; the launch traced here: 47.9 us
  Pallas kernels  45.4 us (94%)
  local copies, waits for them, and re-layouts  1.88 us (4%)
  between operations  0.67 us (1%)
    pallas_call x1, Pallas kernels, on_device(): pl.pallas_call(offer_kernel, name='offer', out_shape=made, in_specs=[HBM]...  20.3 us
    pallas_call x1, Pallas kernels, on_device(): pl.pallas_call(home_kernel, name='home', out_shape=made, in_specs=[HBM] *...  15.2 us
    pallas_call x1, Pallas kernels, on_device(): pl.pallas_call(pairs_kernel, name='pairs', out_shape=made, in_specs=[HBM]...  9.86 us
    unnamed x4, local copies, waits for them, and re-layouts  1.88 us

profile of v3, /device:TPU:1, one launch (start us, length us, event | category | flops | bytes accessed | tf_op | source)
XLA Modules:
  0.0 47.9 jit_solution(5687128122568662203)
XLA Ops:
  0.6 20.3 %offer.1 = (f32[8,512]{1,0:T(8,128)}, bf16[128,256]{1,0:T(8,128)(2,1)}, bf16[128,256]{1,0:T(8,128)(2,1)}, bf16[7,72,256]{2,1,0:T(8,128)(2,1)}, s32[160,128]{1,0:...) custom-call(f32[3,512]{1,0:T(4,128)} %pos_hbm.1, bf16[64,512]{1,0:T(8,128)(2,1)} %feat_hbm.1, ...), custom_call_target="tpu_custom_call" | custom-call | tf_op jit(solution)/shard_map/offer/pallas_call | solution.py:415
  20.9 9.9 %pairs.1 = (f32[32,128]{1,0:T(8,128)}, f32[32,128]{1,0:T(8,128)}, f32[7,8,256]{2,1,0:T(8,128)}) custom-call(f32[8,512]{1,0:T(8,128)} %get-tuple-element.15.own_hbm, bf16[128,256]{1,0:T(8,128)(2,1)} %get-tuple-element.16.left_hbm, bf16[128,256]{1,0:T(8,128)(2,1)} %get-tuple-element.17.right_hbm, bf16[7,72,256]{2,1,0:T(8,128)(2,1)} %get-tuple-element.19.ghost_hbm, ...), custom_call_target="tpu_custom_call" | custom-call | tf_op jit(solution)/shard_map/pairs/pallas_call | solution.py:429
  30.8 15.2 %home.1 = (f32[3,512]{1,0:T(4,128)}, f32[1,512]{1,0:T(1,128)}) custom-call(f32[8,512]{1,0:T(8,128)} %get-tuple-element.15.own_hbm, bf16[128,256]{1,0:T(8,128)(2,1)} %get-tuple-element.16.left_hbm, bf16[128,256]{1,0:T(8,128)(2,1)} %get-tuple-element.17.right_hbm, s32[160,128]{1,0:T(8,128)} %get-tuple-element.18.packed_hbm, ...), custom_call_target="tpu_custom_call" | custom-call | tf_op jit(solution)/shard_map/home/pallas_call | solution.py:444
  46.0 0.0 copy-start
  46.0 1.3 %copy.21 = f32[3,512]{1,0:T(4,128)} copy(f32[3,512]{1,0:T(4,128)} %get-tuple-element.30) | data formatting | bytes 12288
  47.3 0.0 copy-done
  47.3 0.6 %copy.22 = f32[512]{0:T(512)} copy(f32[512]{0:T(512)S(1)} %bitcast.27) | data formatting | bytes 4096
Async XLA Ops:
  46.0 1.3 %copy-start = (f32[1,512]{1,0:T(1,128)S(1)}, f32[1,512]{1,0:T(1,128)}, u32[]{:S(2)}) copy-start(f32[1,512]{1,0:T(1,128)} %get-tuple-element.27) | copy-start | bytes 6148

commit v4 on v3

--- a/solution.py
+++ b/solution.py
@@ -17,10 +17,10 @@
 LIVE = 128
 ROWS = 72
 EARLY = 8
-LATE = 4
+LATE = 8
 HALVES = 4
-U = 2
-LAG = 0
+MANY = 4
+FEW = 2
 
 
 def neighbour(offset, sign):
@@ -93,7 +93,7 @@
         live[at, :] = jnp.where(alive, 1.0, 0.0)
         words[at, :] = jnp.where(alive, (own << 8) + (partner << 17) + LIVE, 0)
         return carry
-    lax.fori_loop(0, rows // 8, find, 0, unroll=4)
+    lax.fori_loop(0, rows // 8, find, 0, unroll=True)
     above = jnp.where(lax.broadcasted_iota(I32, (128, 128), 0) < lax.broadcasted_iota(I32, (128, 128), 1), 1.0, 0.0)
     adder = jnp.concatenate([above, jnp.ones((128, 128), F32)], 1).astype(BF16)
     ranks[0:rows, :] = jnp.dot(live[0:rows, :].astype(BF16), adder, preferred_element_type=F32)
@@ -148,7 +148,7 @@
 
 
 def pair_step(packed, own_tab, tab, chunks, n, left_tab, right_tab, w_mids, w_lasts, w_radials, w_out,
-              hot_own, hot_par, quant, acc_own, acc_par):
+              hot_own, hot_par, quant, acc_own, acc_par, width):
     nb = 8
     centers = lax.broadcasted_iota(I32, (nb, 128), 0).astype(F32) / (nb - 1)
     zero = jnp.zeros((), BF16)
@@ -219,23 +219,15 @@
         acc_par[...] += lax.dot_general(jnp.concatenate(a_par, 1).astype(BF16), hot_par[u], NT, preferred_element_type=F32)
 
     def step(t, carry):
-        streams = [stages(U * t + u, u) for u in range(U)]
-        done, clock = 0, 0
-        while done < U:
-            for u, stream in enumerate(streams):
-                if stream is not None and clock >= LAG * u:
-                    try:
-                        next(stream)
-                    except StopIteration:
-                        streams[u] = None
-                        done += 1
-            clock += 1
+        streams = [stages(width * t + u, u) for u in range(width)]
+        while streams:
+            streams = [stream for stream in streams if next(stream, True) is None]
         return carry
     return step
 
 
 def trips(stand):
-    return (jnp.max(stand) + 128 * U - 1) // (128 * U)
+    return (jnp.max(stand) + 128 * FEW - 1) // (128 * FEW)
 
 
 def offer_kernel(pos_hbm, feat_hbm, species_hbm, scale_hbm, first_hbm, second_hbm, send_hbm,
@@ -244,7 +236,7 @@
                  pos, feat, species, scale, first, second, send, one, two, mask, radial, mid, last, out,
                  offered, own, left_tab, right_tab, packed, stand, acc_own, acc_loc,
                  own_tab, words, live, ranks, hot_own, hot_par, quant, w_mids, w_lasts, w_radials,
-                 in_sem, out_sem, send_sem, recv_sem):
+                 in_sem, out_sem, last_sem, send_sem, recv_sem):
     paths = [OFFSETS[k] for k in DIRECT]
     barrier = meet(paths, 1)
     loads = move((pos_hbm, feat_hbm, species_hbm, scale_hbm, first_hbm, second_hbm, send_hbm,
@@ -291,10 +283,10 @@
     acc_own[...] = jnp.zeros_like(acc_own)
     acc_loc[...] = jnp.zeros_like(acc_loc)
     step = pair_step(packed, own_tab, own_tab, chunks, chunks, left_tab, right_tab, w_mids, w_lasts, w_radials, w_out,
-                     hot_own, hot_par, quant, acc_own, acc_loc)
-    lax.fori_loop(0, EARLY // U, step, 0)
-    stores = move((own, left_tab, right_tab, packed, stand, acc_own, acc_loc),
-                  (own_out, left_out, right_out, packed_out, stand_out, acc_own_out, acc_loc_out), out_sem)
+                     hot_own, hot_par, quant, acc_own, acc_loc, MANY)
+    stores = move((own, left_tab, right_tab, packed, stand), (own_out, left_out, right_out, packed_out, stand_out), out_sem)
+    lax.fori_loop(0, EARLY // MANY, step, 0)
+    stores += move((acc_own, acc_loc), (acc_own_out, acc_loc_out), last_sem)
     copies[0].wait_send()
     finish(copies[1:])
     finish(relays)
@@ -306,12 +298,12 @@
                  acc_own_out, acc_loc_out, force_out,
                  own, left_tab, right_tab, ghost, packed, stand, acc_own, acc_loc, one, two, mask, radial, mid, last, out,
                  own_tab, ghost_tab, gtable, gpacked, words, live, ranks, hot_own, hot_par, quant, acc_gho, force,
-                 w_mids, w_lasts, w_radials, in_sem, out_sem):
+                 w_mids, w_lasts, w_radials, in_sem, out_sem, last_sem):
     loads = move((own_hbm, ghost_hbm, one_hbm, two_hbm, mask_hbm, left_hbm, right_hbm, packed_hbm, stand_hbm,
                   acc_own_hbm, acc_loc_hbm, radial_hbm, mid_hbm, last_hbm, out_hbm),
                  (own, ghost, one, two, mask, left_tab, right_tab, packed, stand,
                   acc_own, acc_loc, radial, mid, last, out), in_sem)
-    finish(loads)
+    finish(loads[0:5])
     count = own.shape[1]
     chunks = count // 128
     sends = ghost.shape[2]
@@ -325,50 +317,51 @@
         for c in range(4):
             row = tail[c:c + 1] + tail[c + 3:c + 4] + float(offset[c]) if c < 3 else tail[6:7]
             spread(row, ghost_tab, c * gchunks + k * per)
+    finish(loads[5:])
     w_out = weights(radial, mid, last, out, w_mids, w_lasts, w_radials)
     gstand = compact(one, two, mask, own_tab, ghost_tab, chunks, gchunks, words, live, ranks, gpacked)
     acc_gho[...] = jnp.zeros_like(acc_gho)
     gstep = pair_step(gpacked, own_tab, ghost_tab, chunks, gchunks, left_tab, gtable, w_mids, w_lasts, w_radials, w_out,
-                      hot_own, hot_par, quant, acc_own, acc_gho)
+                      hot_own, hot_par, quant, acc_own, acc_gho, FEW)
     lax.fori_loop(0, trips(gstand), gstep, 0)
     for ch in range(gchunks):
         cols = slice(128 * (ch % per), 128 * (ch % per) + 128)
         force[ch // per, 0:4, cols] = acc_gho[8 * ch:8 * ch + 4, :] + acc_gho[8 * ch + 4:8 * ch + 8, :]
         force[ch // per, 4:8, cols] = jnp.zeros((4, 128), F32)
     step = pair_step(packed, own_tab, own_tab, chunks, chunks, left_tab, right_tab, w_mids, w_lasts, w_radials, w_out,
-                     hot_own, hot_par, quant, acc_own, acc_loc)
-    lax.fori_loop((EARLY + LATE) // U, trips(stand[...]), step, 0)
-    finish(move((acc_own, acc_loc, force), (acc_own_out, acc_loc_out, force_out), out_sem))
+                     hot_own, hot_par, quant, acc_own, acc_loc, FEW)
+    stores = move((force,), (force_out,), out_sem)
+    lax.fori_loop((EARLY + LATE) // FEW, trips(stand[...]), step, 0)
+    finish(stores + move((acc_own, acc_loc), (acc_own_out, acc_loc_out), last_sem))
 
 
 def home_kernel(own_hbm, left_hbm, right_hbm, packed_hbm, acc_own_hbm, acc_loc_hbm, force_hbm, send_hbm,
                 radial_hbm, mid_hbm, last_hbm, out_hbm,
-                force_out, energy_out,
-                own, left_tab, right_tab, packed, acc_own, acc_loc, force, send, radial, mid, last, out,
-                arrived, own_tab, hot_own, hot_par, quant, w_mids, w_lasts, w_radials, result, energy,
+                result_out,
+                own, left_tab, right_tab, packed, acc_own, acc_loc, send, radial, mid, last, out,
+                arrived, own_tab, hot_own, hot_par, quant, w_mids, w_lasts, w_radials, result,
                 in_sem, out_sem, send_sem, recv_sem):
     barrier = meet(OFFSETS, -1)
-    loads = move((force_hbm, own_hbm, left_hbm, right_hbm, packed_hbm, acc_own_hbm, acc_loc_hbm, send_hbm,
+    loads = move((own_hbm, left_hbm, right_hbm, packed_hbm, acc_own_hbm, acc_loc_hbm, send_hbm,
                   radial_hbm, mid_hbm, last_hbm, out_hbm),
-                 (force, own, left_tab, right_tab, packed, acc_own, acc_loc, send, radial, mid, last, out), in_sem)
-    loads[0].wait()
+                 (own, left_tab, right_tab, packed, acc_own, acc_loc, send, radial, mid, last, out), in_sem)
     pl.semaphore_wait(barrier, len(OFFSETS))
     copies = []
     for k, offset in enumerate(OFFSETS):
         copy = pltpu.make_async_remote_copy(
-            src_ref=force.at[k], dst_ref=arrived.at[k], send_sem=send_sem.at[k], recv_sem=recv_sem.at[k],
+            src_ref=force_hbm.at[k], dst_ref=arrived.at[k], send_sem=send_sem.at[k], recv_sem=recv_sem.at[k],
             device_id=neighbour(offset, 1), device_id_type=MESH_IDS)
         copy.start()
         copies.append(copy)
-    finish(loads[1:])
+    finish(loads)
     count = own.shape[1]
     chunks = count // 128
     for c in range(4):
         spread(own[c:c + 1, :], own_tab, c * chunks)
     w_out = weights(radial, mid, last, out, w_mids, w_lasts, w_radials)
     step = pair_step(packed, own_tab, own_tab, chunks, chunks, left_tab, right_tab, w_mids, w_lasts, w_radials, w_out,
-                     hot_own, hot_par, quant, acc_own, acc_loc)
-    lax.fori_loop(EARLY // U, (EARLY + LATE) // U, step, 0)
+                     hot_own, hot_par, quant, acc_own, acc_loc, MANY)
+    lax.fori_loop(EARLY // MANY, (EARLY + LATE) // MANY, step, 0)
     hot = one_hot(send[...], count)
     finish(copies)
     total = arrived[0]
@@ -383,9 +376,9 @@
         cols = slice(128 * ch, 128 * ch + 128)
         mine = acc_own[8 * ch:8 * ch + 4, :] + acc_own[8 * ch + 4:8 * ch + 8, :]
         other = acc_loc[8 * ch:8 * ch + 4, :] + acc_loc[8 * ch + 4:8 * ch + 8, :]
-        result[:, cols] = mine[0:3] - other[0:3] - back[0:3, cols]
-        energy[:, cols] = mine[3:4]
-    finish(move((result, energy), (force_out, energy_out), out_sem))
+        result[0:3, cols] = mine[0:3] - other[0:3] - back[0:3, cols]
+        result[3:4, cols] = mine[3:4]
+    finish(move((result,), (result_out,), out_sem))
 
 
 def on_device(positions, features, species, species_scale, w_first, w_second, w_radial, w_mid, w_last, w_out,
@@ -404,7 +397,7 @@
     local = [x.reshape(lrows, 128) for x in (local_first, local_second, local_mask)]
     ghostly = [x.reshape(grows, 128) for x in (ghost_owner, ghost_index, ghost_mask)]
     blocks_w = [v((4 * channels, 4 * channels), BF16), v((4 * channels, 4 * channels), BF16), v((4 * channels, 16 * nb), BF16)]
-    hots = [v((U, 128, 1024), BF16), v((U, 128, 1024), BF16), v((U, 64, 128), F32)]
+    hots = lambda width: [v((width, 128, 1024), BF16), v((width, 128, 1024), BF16), v((width, 64, 128), F32)]
     table = shape((channels * count // 256, 256), BF16)
     acc = shape((8 * chunks, 128), F32)
     own_tab = v((4 * chunks, 8, 128), F32)
@@ -419,8 +412,8 @@
         in_specs=[HBM] * len(args),
         out_specs=[HBM] * len(made),
         scratch_shapes=buffers(args) + [v((ROWS, sends), BF16)] + buffers(made[0:3] + made[4:]) + [
-            own_tab, v((lrows, 128), I32), v((lrows, 128), F32), v((lrows, 256), F32)] + hots + blocks_w + [
-            sems(len(args)), sems(len(made) - 1), sems(blocks), sems(blocks)],
+            own_tab, v((lrows, 128), I32), v((lrows, 128), F32), v((lrows, 256), F32)] + hots(MANY) + blocks_w + [
+            sems(len(args)), sems(5), sems(2), sems(blocks), sems(blocks)],
         compiler_params=pltpu.CompilerParams(collective_id=0, has_side_effects=True, vmem_limit_bytes=60 << 20),
     )(*args)
 
@@ -434,24 +427,24 @@
         out_specs=[HBM] * len(made),
         scratch_shapes=buffers(args) + [
             own_tab, v((4 * gchunks, 8, 128), F32), v((channels * gchunks // 2, 256), BF16), v((grows, 128), I32),
-            v((grows, 128), I32), v((grows, 128), F32), v((grows, 256), F32)] + hots + [
-            v((8 * gchunks, 128), F32), v((blocks, 8, sends), F32)] + blocks_w + [sems(len(args)), sems(len(made))],
+            v((grows, 128), I32), v((grows, 128), F32), v((grows, 256), F32)] + hots(FEW) + [
+            v((8 * gchunks, 128), F32), v((blocks, 8, sends), F32)] + blocks_w + [sems(len(args)), sems(1), sems(2)],
         compiler_params=pltpu.CompilerParams(vmem_limit_bytes=60 << 20),
     )(*args)
 
     args = [own, left_tab, right_tab, packed, acc_own, acc_loc, gforce, send_row] + net
-    made = [shape((3, count), F32), shape((1, count), F32)]
-    forces, energy = pl.pallas_call(
+    made = [shape((4, count), F32)]
+    result, = pl.pallas_call(
         home_kernel,
         name="home",
         out_shape=made,
         in_specs=[HBM] * len(args),
         out_specs=[HBM] * len(made),
-        scratch_shapes=buffers(args) + [v((blocks, 8, sends), F32), own_tab] + hots + blocks_w + buffers(made) + [
-            sems(len(args)), sems(len(made)), sems(blocks), sems(blocks)],
+        scratch_shapes=buffers(args[:6] + args[7:]) + [v((blocks, 8, sends), F32), own_tab] + hots(MANY) + blocks_w + buffers(made) + [
+            sems(len(args) - 1), sems(len(made)), sems(blocks), sems(blocks)],
         compiler_params=pltpu.CompilerParams(collective_id=1, has_side_effects=True, vmem_limit_bytes=60 << 20),
     )(*args)
-    return forces, energy.reshape(count)
+    return result[0:3], result[3]
 
 
 def solution(mesh):

time: 48.2 us -> 43.5 us (0.902)
  Pallas kernels: 45.4 us -> 39.8 us
  local copies, waits for them, and re-layouts: 1.88 us -> 2.57 us
    pallas_call x1, Pallas kernels: 9.86 us -> 5.95 us  [on_device(): pl.pallas_call(pairs_kernel, name='pairs', out_shape=made, in_specs=[HBM]...]
    pallas_call x1, Pallas kernels: 20.3 us -> 18.8 us  [on_device(): pl.pallas_call(offer_kernel, name='offer', out_shape=made, in_specs=[HBM]...]
    slice x0 -> x1, local copies, waits for them, and re-layouts: none -> 1.28 us  [on_device(): return (result[0:3], result[3])]
    unnamed x4 -> x1, local copies, waits for them, and re-layouts: 1.88 us -> 1.3 us
where the time goes in v4:
time: 43.5 us; the launch traced here: 43 us
  Pallas kernels  39.8 us (91%)
  local copies, waits for them, and re-layouts  2.57 us (6%)
  between operations  0.66 us (2%)
    pallas_call x1, Pallas kernels, on_device(): pl.pallas_call(offer_kernel, name='offer', out_shape=made, in_specs=[HBM]...  18.8 us
    pallas_call x1, Pallas kernels, on_device(): pl.pallas_call(home_kernel, name='home', out_shape=made, in_specs=[HBM] *...  15 us
    pallas_call x1, Pallas kernels, on_device(): pl.pallas_call(pairs_kernel, name='pairs', out_shape=made, in_specs=[HBM]...  5.95 us
    unnamed x1, local copies, waits for them, and re-layouts  1.3 us
    slice x1, local copies, waits for them, and re-layouts, on_device(): return (result[0:3], result[3])  1.28 us

profile of v4, /device:TPU:1, one launch (start us, length us, event | category | flops | bytes accessed | tf_op | source)
XLA Modules:
  0.0 43.0 jit_solution(17255023266671999173)
XLA Ops:
  0.6 18.8 %offer.1 = (f32[8,512]{1,0:T(8,128)}, bf16[128,256]{1,0:T(8,128)(2,1)}, bf16[128,256]{1,0:T(8,128)(2,1)}, bf16[7,72,256]{2,1,0:T(8,128)(2,1)}, s32[160,128]{1,0:...) custom-call(f32[3,512]{1,0:T(4,128)} %pos_hbm.1, bf16[64,512]{1,0:T(8,128)(2,1)} %feat_hbm.1, ...), custom_call_target="tpu_custom_call" | custom-call | tf_op jit(solution)/shard_map/offer/pallas_call | solution.py:408
  19.4 5.9 %pairs.1 = (f32[32,128]{1,0:T(8,128)}, f32[32,128]{1,0:T(8,128)}, f32[7,8,256]{2,1,0:T(8,128)}) custom-call(f32[8,512]{1,0:T(8,128)} %get-tuple-element.13.own_hbm, bf16[128,256]{1,0:T(8,128)(2,1)} %get-tuple-element.14.left_hbm, bf16[128,256]{1,0:T(8,128)(2,1)} %get-tuple-element.15.right_hbm, bf16[7,72,256]{2,1,0:T(8,128)(2,1)} %get-tuple-element.17.ghost_hbm, ...), custom_call_target="tpu_custom_call" | custom-call | tf_op jit(solution)/shard_map/pairs/pallas_call | solution.py:422
  25.4 15.0 %home.1 = f32[4,512]{1,0:T(4,128)} custom-call(f32[8,512]{1,0:T(8,128)} %get-tuple-element.13.own_hbm, bf16[128,256]{1,0:T(8,128)(2,1)} %get-tuple-element.14.left_hbm, bf16[128,256]{1,0:T(8,128)(2,1)} %get-tuple-element.15.right_hbm, s32[160,128]{1,0:T(8,128)} %get-tuple-element.16.packed_hbm, f32[32,128]{1,0:T(8,128)} %get-tuple-element.21.acc_own_hbm, ...), custom_call_target="tpu_custom_call" | custom-call | tf_op jit(solution)/shard_map/home/pallas_call | solution.py:437
  40.4 1.3 %slice.7 = f32[1,512]{1,0:T(1,128)} slice(f32[4,512]{1,0:T(4,128)} %home.1), slice={[3:4], [0:512]} | slice | bytes 4096 | tf_op jit(solution)/shard_map/slice | solution.py:447
  41.7 1.3 %copy.20 = f32[3,512]{1,0:T(4,128)} copy(f32[3,512]{1,0:T(4,128)} %bitcast.19) | data formatting | bytes 12288

commit v5 on v4

--- a/solution.py
+++ b/solution.py
@@ -161,7 +161,7 @@
 
         def gather(low, high, keep, table, groups, half):
             hot = one_hot(wide(low, half), 128)
-            keep[u, :, 256 * half:256 * half + 256] = hot
+            keep[u, :, 256 * half:256 * half + 256] = hot[0:64] + hot[64:128]
             top = wide(high, half)
             odd = jnp.broadcast_to((top & 1).astype(jnp.int16), (128, 256))
             hot = jnp.concatenate([jnp.where(odd == jnp.int16(0), hot, zero), jnp.where(odd == jnp.int16(1), hot, zero)], 0)
@@ -211,10 +211,11 @@
             quant[u, 8 * q:8 * q + 8, :] = high
             quant[u, 32 + 8 * q:40 + 8 * q, :] = low
         a_own, a_par = [], []
+        part_i, part_j = own >> 6, partner >> 6
         for r in range(8):
             tile = quant[u, pl.ds(r, 8, stride=8), :]
-            a_own.append(jnp.concatenate([jnp.where(high_i[r:r + 1] == ch, tile, 0.0) for ch in range(chunks)], 0))
-            a_par.append(jnp.concatenate([jnp.where(high_j[r:r + 1] == ch, tile, 0.0) for ch in range(n)], 0))
+            a_own.append(jnp.concatenate([jnp.where(part_i[r:r + 1] == ch, tile, 0.0) for ch in range(2 * chunks)], 0))
+            a_par.append(jnp.concatenate([jnp.where(part_j[r:r + 1] == ch, tile, 0.0) for ch in range(2 * n)], 0))
         acc_own[...] += lax.dot_general(jnp.concatenate(a_own, 1).astype(BF16), hot_own[u], NT, preferred_element_type=F32)
         acc_par[...] += lax.dot_general(jnp.concatenate(a_par, 1).astype(BF16), hot_par[u], NT, preferred_element_type=F32)
 
@@ -224,6 +225,10 @@
             streams = [stream for stream in streams if next(stream, True) is None]
         return carry
     return step
+
+
+def joined(acc, ch):
+    return jnp.concatenate([acc[8 * k:8 * k + 4, :] + acc[8 * k + 4:8 * k + 8, :] for k in (2 * ch, 2 * ch + 1)], 1)
 
 
 def trips(stand):
@@ -277,9 +282,9 @@
         spread(own[c:c + 1, :], own_tab, c * chunks)
     finish(loads[7:])
     w_out = weights(radial, mid, last, out, w_mids, w_lasts, w_radials)
+    stand[...] = compact(one, two, mask, own_tab, own_tab, chunks, chunks, words, live, ranks, packed)
     copies[0].wait_recv()
     relays = [remote(ghost_out.at[2], k, OFFSETS[step]) for step, k in RELAYED]
-    stand[...] = compact(one, two, mask, own_tab, own_tab, chunks, chunks, words, live, ranks, packed)
     acc_own[...] = jnp.zeros_like(acc_own)
     acc_loc[...] = jnp.zeros_like(acc_loc)
     step = pair_step(packed, own_tab, own_tab, chunks, chunks, left_tab, right_tab, w_mids, w_lasts, w_radials, w_out,
@@ -326,7 +331,7 @@
     lax.fori_loop(0, trips(gstand), gstep, 0)
     for ch in range(gchunks):
         cols = slice(128 * (ch % per), 128 * (ch % per) + 128)
-        force[ch // per, 0:4, cols] = acc_gho[8 * ch:8 * ch + 4, :] + acc_gho[8 * ch + 4:8 * ch + 8, :]
+        force[ch // per, 0:4, cols] = joined(acc_gho, ch)
         force[ch // per, 4:8, cols] = jnp.zeros((4, 128), F32)
     step = pair_step(packed, own_tab, own_tab, chunks, chunks, left_tab, right_tab, w_mids, w_lasts, w_radials, w_out,
                      hot_own, hot_par, quant, acc_own, acc_loc, FEW)
@@ -335,35 +340,40 @@
     finish(stores + move((acc_own, acc_loc), (acc_own_out, acc_loc_out), last_sem))
 
 
-def home_kernel(own_hbm, left_hbm, right_hbm, packed_hbm, acc_own_hbm, acc_loc_hbm, force_hbm, send_hbm,
+def home_kernel(own_hbm, left_hbm, right_hbm, packed_hbm, acc_own_hbm, acc_loc_hbm, force_hbm,
                 radial_hbm, mid_hbm, last_hbm, out_hbm,
-                result_out,
-                own, left_tab, right_tab, packed, acc_own, acc_loc, send, radial, mid, last, out,
-                arrived, own_tab, hot_own, hot_par, quant, w_mids, w_lasts, w_radials, result,
+                acc_own_out, acc_loc_out, arrived_out,
+                own, left_tab, right_tab, packed, acc_own, acc_loc, radial, mid, last, out,
+                own_tab, hot_own, hot_par, quant, w_mids, w_lasts, w_radials,
                 in_sem, out_sem, send_sem, recv_sem):
     barrier = meet(OFFSETS, -1)
-    loads = move((own_hbm, left_hbm, right_hbm, packed_hbm, acc_own_hbm, acc_loc_hbm, send_hbm,
-                  radial_hbm, mid_hbm, last_hbm, out_hbm),
-                 (own, left_tab, right_tab, packed, acc_own, acc_loc, send, radial, mid, last, out), in_sem)
+    finish(move((own_hbm, left_hbm, right_hbm, packed_hbm, acc_own_hbm, acc_loc_hbm, radial_hbm, mid_hbm, last_hbm, out_hbm),
+                (own, left_tab, right_tab, packed, acc_own, acc_loc, radial, mid, last, out), in_sem))
     pl.semaphore_wait(barrier, len(OFFSETS))
     copies = []
     for k, offset in enumerate(OFFSETS):
         copy = pltpu.make_async_remote_copy(
-            src_ref=force_hbm.at[k], dst_ref=arrived.at[k], send_sem=send_sem.at[k], recv_sem=recv_sem.at[k],
+            src_ref=force_hbm.at[k], dst_ref=arrived_out.at[k], send_sem=send_sem.at[k], recv_sem=recv_sem.at[k],
             device_id=neighbour(offset, 1), device_id_type=MESH_IDS)
         copy.start()
         copies.append(copy)
-    finish(loads)
-    count = own.shape[1]
-    chunks = count // 128
+    chunks = own.shape[1] // 128
     for c in range(4):
         spread(own[c:c + 1, :], own_tab, c * chunks)
     w_out = weights(radial, mid, last, out, w_mids, w_lasts, w_radials)
     step = pair_step(packed, own_tab, own_tab, chunks, chunks, left_tab, right_tab, w_mids, w_lasts, w_radials, w_out,
                      hot_own, hot_par, quant, acc_own, acc_loc, MANY)
     lax.fori_loop(EARLY // MANY, (EARLY + LATE) // MANY, step, 0)
+    stores = move((acc_own, acc_loc), (acc_own_out, acc_loc_out), out_sem)
+    finish(copies)
+    finish(stores)
+
+
+def join_kernel(acc_own_hbm, acc_loc_hbm, arrived_hbm, send_hbm, force_out, energy_out,
+                acc_own, acc_loc, arrived, send, result, energy, in_sem, out_sem):
+    finish(move((acc_own_hbm, acc_loc_hbm, arrived_hbm, send_hbm), (acc_own, acc_loc, arrived, send), in_sem))
+    count = result.shape[1]
     hot = one_hot(send[...], count)
-    finish(copies)
     total = arrived[0]
     for k in range(1, len(OFFSETS)):
         total = total + arrived[k]
@@ -372,13 +382,12 @@
     parts = jnp.concatenate([high, mid_part, low, jnp.zeros_like(low)], 0).astype(BF16)
     back = lax.dot_general(parts, hot, NT, preferred_element_type=F32)
     back = back[0:8] + back[8:16] + back[16:24]
-    for ch in range(chunks):
+    for ch in range(count // 128):
         cols = slice(128 * ch, 128 * ch + 128)
-        mine = acc_own[8 * ch:8 * ch + 4, :] + acc_own[8 * ch + 4:8 * ch + 8, :]
-        other = acc_loc[8 * ch:8 * ch + 4, :] + acc_loc[8 * ch + 4:8 * ch + 8, :]
-        result[0:3, cols] = mine[0:3] - other[0:3] - back[0:3, cols]
-        result[3:4, cols] = mine[3:4]
-    finish(move((result,), (result_out,), out_sem))
+        mine = joined(acc_own, ch)
+        result[:, cols] = mine[0:3] - joined(acc_loc, ch)[0:3] - back[0:3, cols]
+        energy[:, cols] = mine[3:4]
+    finish(move((result, energy), (force_out, energy_out), out_sem))
 
 
 def on_device(positions, features, species, species_scale, w_first, w_second, w_radial, w_mid, w_last, w_out,
@@ -397,9 +406,9 @@
     local = [x.reshape(lrows, 128) for x in (local_first, local_second, local_mask)]
     ghostly = [x.reshape(grows, 128) for x in (ghost_owner, ghost_index, ghost_mask)]
     blocks_w = [v((4 * channels, 4 * channels), BF16), v((4 * channels, 4 * channels), BF16), v((4 * channels, 16 * nb), BF16)]
-    hots = lambda width: [v((width, 128, 1024), BF16), v((width, 128, 1024), BF16), v((width, 64, 128), F32)]
+    hots = lambda width: [v((width, 64, 1024), BF16), v((width, 64, 1024), BF16), v((width, 64, 128), F32)]
     table = shape((channels * count // 256, 256), BF16)
-    acc = shape((8 * chunks, 128), F32)
+    acc = shape((16 * chunks, 64), F32)
     own_tab = v((4 * chunks, 8, 128), F32)
 
     args = [positions, features, species.reshape(1, count), species_scale.reshape(1, -1), w_first, w_second, send_row] + local + net
@@ -428,23 +437,35 @@
         scratch_shapes=buffers(args) + [
             own_tab, v((4 * gchunks, 8, 128), F32), v((channels * gchunks // 2, 256), BF16), v((grows, 128), I32),
             v((grows, 128), I32), v((grows, 128), F32), v((grows, 256), F32)] + hots(FEW) + [
-            v((8 * gchunks, 128), F32), v((blocks, 8, sends), F32)] + blocks_w + [sems(len(args)), sems(1), sems(2)],
+            v((16 * gchunks, 64), F32), v((blocks, 8, sends), F32)] + blocks_w + [sems(len(args)), sems(1), sems(2)],
         compiler_params=pltpu.CompilerParams(vmem_limit_bytes=60 << 20),
     )(*args)
 
-    args = [own, left_tab, right_tab, packed, acc_own, acc_loc, gforce, send_row] + net
-    made = [shape((4, count), F32)]
-    result, = pl.pallas_call(
+    args = [own, left_tab, right_tab, packed, acc_own, acc_loc, gforce] + net
+    made = [acc, acc, shape((blocks, 8, sends), F32)]
+    acc_own, acc_loc, arrived = pl.pallas_call(
         home_kernel,
         name="home",
         out_shape=made,
         in_specs=[HBM] * len(args),
         out_specs=[HBM] * len(made),
-        scratch_shapes=buffers(args[:6] + args[7:]) + [v((blocks, 8, sends), F32), own_tab] + hots(MANY) + blocks_w + buffers(made) + [
-            sems(len(args) - 1), sems(len(made)), sems(blocks), sems(blocks)],
+        scratch_shapes=buffers(args[:6] + args[7:]) + [own_tab] + hots(MANY) + blocks_w + [
+            sems(len(args) - 1), sems(2), sems(blocks), sems(blocks)],
         compiler_params=pltpu.CompilerParams(collective_id=1, has_side_effects=True, vmem_limit_bytes=60 << 20),
     )(*args)
-    return result[0:3], result[3]
+
+    args = [acc_own, acc_loc, arrived, send_row]
+    made = [shape((3, count), F32), shape((1, count), F32)]
+    forces, energy = pl.pallas_call(
+        join_kernel,
+        name="join",
+        out_shape=made,
+        in_specs=[HBM] * len(args),
+        out_specs=[HBM] * len(made),
+        scratch_shapes=buffers(args) + buffers(made) + [sems(len(args)), sems(len(made))],
+        compiler_params=pltpu.CompilerParams(vmem_limit_bytes=60 << 20),
+    )(*args)
+    return forces, energy.reshape(count)
 
 
 def solution(mesh):

time: 43.5 us -> 40.6 us (0.933)
  local copies, waits for them, and re-layouts: 2.57 us -> 0 us
    pallas_call x1, Pallas kernels: 18.8 us -> 16.6 us  [on_device(): pl.pallas_call(offer_kernel, name='offer', out_shape=made, in_specs=[HBM]...]
    pallas_call x1, Pallas kernels: 5.95 us -> 8.04 us  [on_device(): pl.pallas_call(pairs_kernel, name='pairs', out_shape=made, in_specs=[HBM]...]
    pallas_call x1, Pallas kernels: 15 us -> 13.3 us  [on_device(): pl.pallas_call(home_kernel, name='home', out_shape=made, in_specs=[HBM] *...]
    pallas_call x0 -> x1, Pallas kernels: none -> 1.71 us  [on_device(): pl.pallas_call(join_kernel, name='join', out_shape=made, in_specs=[HBM] *...]
    unnamed x1 -> x0, local copies, waits for them, and re-layouts: 1.3 us -> none
    slice x1 -> x0, local copies, waits for them, and re-layouts: 1.28 us -> none  [on_device(): return (result[0:3], result[3])]
where the time goes in v5:
time: 40.6 us; the launch traced here: 40.2 us
  Pallas kernels  39.6 us (98%)
  between operations  0.66 us (2%)
    pallas_call x1, Pallas kernels, on_device(): pl.pallas_call(offer_kernel, name='offer', out_shape=made, in_specs=[HBM]...  16.6 us
    pallas_call x1, Pallas kernels, on_device(): pl.pallas_call(home_kernel, name='home', out_shape=made, in_specs=[HBM] *...  13.3 us
    pallas_call x1, Pallas kernels, on_device(): pl.pallas_call(pairs_kernel, name='pairs', out_shape=made, in_specs=[HBM]...  8.04 us
    pallas_call x1, Pallas kernels, on_device(): pl.pallas_call(join_kernel, name='join', out_shape=made, in_specs=[HBM] *...  1.71 us

profile of v5, /device:TPU:1, one launch (start us, length us, event | category | flops | bytes accessed | tf_op | source)
XLA Modules:
  0.0 40.2 jit_solution(7272338598089450709)
XLA Ops:
  0.6 16.6 %offer.1 = (f32[8,512]{1,0:T(8,128)}, bf16[128,256]{1,0:T(8,128)(2,1)}, bf16[128,256]{1,0:T(8,128)(2,1)}, bf16[7,72,256]{2,1,0:T(8,128)(2,1)}, s32[160,128]{1,0:...) custom-call(f32[3,512]{1,0:T(4,128)} %pos_hbm.1, bf16[64,512]{1,0:T(8,128)(2,1)} %feat_hbm.1, ...), custom_call_target="tpu_custom_call" | custom-call | tf_op jit(solution)/shard_map/offer/pallas_call | solution.py:417
  17.2 8.0 %pairs.1 = (f32[64,64]{1,0:T(8,128)}, f32[64,64]{1,0:T(8,128)}, f32[7,8,256]{2,1,0:T(8,128)}) custom-call(f32[8,512]{1,0:T(8,128)} %get-tuple-element.18.own_hbm, bf16[128,256]{1,0:T(8,128)(2,1)} %get-tuple-element.19.left_hbm, bf16[128,256]{1,0:T(8,128)(2,1)} %get-tuple-element.20.right_hbm, bf16[7,72,256]{2,1,0:T(8,128)(2,1)} %get-tuple-element.22.ghost_hbm, ...), custom_call_target="tpu_custom_call" | custom-call | tf_op jit(solution)/shard_map/pairs/pallas_call | solution.py:431
  25.2 13.3 %home.1 = (f32[64,64]{1,0:T(8,128)}, f32[64,64]{1,0:T(8,128)}, f32[7,8,256]{2,1,0:T(8,128)}) custom-call(f32[8,512]{1,0:T(8,128)} %get-tuple-element.18.own_hbm, bf16[128,256]{1,0:T(8,128)(2,1)} %get-tuple-element.19.left_hbm, bf16[128,256]{1,0:T(8,128)(2,1)} %get-tuple-element.20.right_hbm, s32[160,128]{1,0:T(8,128)} %get-tuple-element.21.packed_hbm, ...), custom_call_target="tpu_custom_call" | custom-call | tf_op jit(solution)/shard_map/home/pallas_call | solution.py:446
  38.5 1.7 %join.1 = (f32[3,512]{1,0:T(4,128)}, f32[1,512]{1,0:T(1,128)}) custom-call(f32[64,64]{1,0:T(8,128)} %get-tuple-element.29.acc_own_hbm, f32[64,64]{1,0:T(8,128)} %get-tuple-element.30.acc_loc_hbm, f32[7,8,256]{2,1,0:T(8,128)} %get-tuple-element.31.arrived_hbm, s32[1,256]{1,0:T(1,128)} %bitcast.25), custom_call_target="tpu_custom_call" | custom-call | tf_op jit(solution)/shard_map/join/pallas_call | solution.py:459

commit v6 on v5

--- a/solution.py
+++ b/solution.py
@@ -21,6 +21,7 @@
 HALVES = 4
 MANY = 4
 FEW = 2
+GHOSTLY = 3
 
 
 def neighbour(offset, sign):
@@ -207,15 +208,16 @@
         slope = weight * (envelope * reslope - 2.0 * near * readout)
         outs = [2.0 * g * slope for g in gap] + [energy]
         for q, out in enumerate(outs):
-            high, low = split_two(out)
-            quant[u, 8 * q:8 * q + 8, :] = high
-            quant[u, 32 + 8 * q:40 + 8 * q, :] = low
+            quant[u, 8 * q:8 * q + 8, :] = out
+            quant[u, 32 + 8 * q:40 + 8 * q, :] = out
         a_own, a_par = [], []
         part_i, part_j = own >> 6, partner >> 6
+        which = lax.broadcasted_iota(I32, (8, 128), 0) >> 2
         for r in range(8):
             tile = quant[u, pl.ds(r, 8, stride=8), :]
-            a_own.append(jnp.concatenate([jnp.where(part_i[r:r + 1] == ch, tile, 0.0) for ch in range(2 * chunks)], 0))
-            a_par.append(jnp.concatenate([jnp.where(part_j[r:r + 1] == ch, tile, 0.0) for ch in range(2 * n)], 0))
+            pick_i, pick_j = part_i[r:r + 1] - which, part_j[r:r + 1] - which
+            a_own.append(jnp.concatenate([jnp.where(pick_i == 2 * ch, tile, 0.0) for ch in range(chunks)], 0))
+            a_par.append(jnp.concatenate([jnp.where(pick_j == 2 * ch, tile, 0.0) for ch in range(n)], 0))
         acc_own[...] += lax.dot_general(jnp.concatenate(a_own, 1).astype(BF16), hot_own[u], NT, preferred_element_type=F32)
         acc_par[...] += lax.dot_general(jnp.concatenate(a_par, 1).astype(BF16), hot_par[u], NT, preferred_element_type=F32)
 
@@ -228,11 +230,11 @@
 
 
 def joined(acc, ch):
-    return jnp.concatenate([acc[8 * k:8 * k + 4, :] + acc[8 * k + 4:8 * k + 8, :] for k in (2 * ch, 2 * ch + 1)], 1)
-
-
-def trips(stand):
-    return (jnp.max(stand) + 128 * FEW - 1) // (128 * FEW)
+    return jnp.concatenate([acc[8 * ch:8 * ch + 4, :], acc[8 * ch + 4:8 * ch + 8, :]], 1)
+
+
+def trips(stand, width):
+    return (jnp.max(stand) + (128 * width - 1)) // (128 * width)
 
 
 def offer_kernel(pos_hbm, feat_hbm, species_hbm, scale_hbm, first_hbm, second_hbm, send_hbm,
@@ -327,8 +329,8 @@
     gstand = compact(one, two, mask, own_tab, ghost_tab, chunks, gchunks, words, live, ranks, gpacked)
     acc_gho[...] = jnp.zeros_like(acc_gho)
     gstep = pair_step(gpacked, own_tab, ghost_tab, chunks, gchunks, left_tab, gtable, w_mids, w_lasts, w_radials, w_out,
-                      hot_own, hot_par, quant, acc_own, acc_gho, FEW)
-    lax.fori_loop(0, trips(gstand), gstep, 0)
+                      hot_own, hot_par, quant, acc_own, acc_gho, GHOSTLY)
+    lax.fori_loop(0, trips(gstand, GHOSTLY), gstep, 0)
     for ch in range(gchunks):
         cols = slice(128 * (ch % per), 128 * (ch % per) + 128)
         force[ch // per, 0:4, cols] = joined(acc_gho, ch)
@@ -336,7 +338,7 @@
     step = pair_step(packed, own_tab, own_tab, chunks, chunks, left_tab, right_tab, w_mids, w_lasts, w_radials, w_out,
                      hot_own, hot_par, quant, acc_own, acc_loc, FEW)
     stores = move((force,), (force_out,), out_sem)
-    lax.fori_loop((EARLY + LATE) // FEW, trips(stand[...]), step, 0)
+    lax.fori_loop((EARLY + LATE) // FEW, trips(stand[...], FEW), step, 0)
     finish(stores + move((acc_own, acc_loc), (acc_own_out, acc_loc_out), last_sem))
 
 
@@ -408,7 +410,7 @@
     blocks_w = [v((4 * channels, 4 * channels), BF16), v((4 * channels, 4 * channels), BF16), v((4 * channels, 16 * nb), BF16)]
     hots = lambda width: [v((width, 64, 1024), BF16), v((width, 64, 1024), BF16), v((width, 64, 128), F32)]
     table = shape((channels * count // 256, 256), BF16)
-    acc = shape((16 * chunks, 64), F32)
+    acc = shape((8 * chunks, 64), F32)
     own_tab = v((4 * chunks, 8, 128), F32)
 
     args = [positions, features, species.reshape(1, count), species_scale.reshape(1, -1), w_first, w_second, send_row] + local + net
@@ -436,8 +438,8 @@
         out_specs=[HBM] * len(made),
         scratch_shapes=buffers(args) + [
             own_tab, v((4 * gchunks, 8, 128), F32), v((channels * gchunks // 2, 256), BF16), v((grows, 128), I32),
-            v((grows, 128), I32), v((grows, 128), F32), v((grows, 256), F32)] + hots(FEW) + [
-            v((16 * gchunks, 64), F32), v((blocks, 8, sends), F32)] + blocks_w + [sems(len(args)), sems(1), sems(2)],
+            v((grows, 128), I32), v((grows, 128), F32), v((grows, 256), F32)] + hots(GHOSTLY) + [
+            v((8 * gchunks, 64), F32), v((blocks, 8, sends), F32)] + blocks_w + [sems(len(args)), sems(1), sems(2)],
         compiler_params=pltpu.CompilerParams(vmem_limit_bytes=60 << 20),
     )(*args)
 

time: 40.6 us -> 38.9 us (0.958)
  Pallas kernels: 39.6 us -> 37.8 us
    pallas_call x1, Pallas kernels: 8.04 us -> 6.52 us  [on_device(): pl.pallas_call(pairs_kernel, name='pairs', out_shape=made, in_specs=[HBM]...]
where the time goes in v6:
time: 38.9 us; the launch traced here: 38.4 us
  Pallas kernels  37.8 us (97%)
  between operations  0.66 us (2%)
    pallas_call x1, Pallas kernels, on_device(): pl.pallas_call(offer_kernel, name='offer', out_shape=made, in_specs=[HBM]...  16.4 us
    pallas_call x1, Pallas kernels, on_device(): pl.pallas_call(home_kernel, name='home', out_shape=made, in_specs=[HBM] *...  13.2 us
    pallas_call x1, Pallas kernels, on_device(): pl.pallas_call(pairs_kernel, name='pairs', out_shape=made, in_specs=[HBM]...  6.52 us
    pallas_call x1, Pallas kernels, on_device(): pl.pallas_call(join_kernel, name='join', out_shape=made, in_specs=[HBM] *...  1.7 us

profile of v6, /device:TPU:1, one launch (start us, length us, event | category | flops | bytes accessed | tf_op | source)
XLA Modules:
  0.0 38.4 jit_solution(10488428857601862378)
XLA Ops:
  0.6 16.4 %offer.1 = (f32[8,512]{1,0:T(8,128)}, bf16[128,256]{1,0:T(8,128)(2,1)}, bf16[128,256]{1,0:T(8,128)(2,1)}, bf16[7,72,256]{2,1,0:T(8,128)(2,1)}, s32[160,128]{1,0:...) custom-call(f32[3,512]{1,0:T(4,128)} %pos_hbm.1, bf16[64,512]{1,0:T(8,128)(2,1)} %feat_hbm.1, ...), custom_call_target="tpu_custom_call" | custom-call | tf_op jit(solution)/shard_map/offer/pallas_call | solution.py:419
  17.1 6.5 %pairs.1 = (f32[32,64]{1,0:T(8,128)}, f32[32,64]{1,0:T(8,128)}, f32[7,8,256]{2,1,0:T(8,128)}) custom-call(f32[8,512]{1,0:T(8,128)} %get-tuple-element.18.own_hbm, bf16[128,256]{1,0:T(8,128)(2,1)} %get-tuple-element.19.left_hbm, bf16[128,256]{1,0:T(8,128)(2,1)} %get-tuple-element.20.right_hbm, bf16[7,72,256]{2,1,0:T(8,128)(2,1)} %get-tuple-element.22.ghost_hbm, ...), custom_call_target="tpu_custom_call" | custom-call | tf_op jit(solution)/shard_map/pairs/pallas_call | solution.py:433
  23.6 13.2 %home.1 = (f32[32,64]{1,0:T(8,128)}, f32[32,64]{1,0:T(8,128)}, f32[7,8,256]{2,1,0:T(8,128)}) custom-call(f32[8,512]{1,0:T(8,128)} %get-tuple-element.18.own_hbm, bf16[128,256]{1,0:T(8,128)(2,1)} %get-tuple-element.19.left_hbm, bf16[128,256]{1,0:T(8,128)(2,1)} %get-tuple-element.20.right_hbm, s32[160,128]{1,0:T(8,128)} %get-tuple-element.21.packed_hbm, ...), custom_call_target="tpu_custom_call" | custom-call | tf_op jit(solution)/shard_map/home/pallas_call | solution.py:448
  36.7 1.7 %join.1 = (f32[3,512]{1,0:T(4,128)}, f32[1,512]{1,0:T(1,128)}) custom-call(f32[32,64]{1,0:T(8,128)} %get-tuple-element.29.acc_own_hbm, f32[32,64]{1,0:T(8,128)} %get-tuple-element.30.acc_loc_hbm, f32[7,8,256]{2,1,0:T(8,128)} %get-tuple-element.31.arrived_hbm, s32[1,256]{1,0:T(1,128)} %bitcast.25), custom_call_target="tpu_custom_call" | custom-call | tf_op jit(solution)/shard_map/join/pallas_call | solution.py:461

commit v7 on v6

--- a/solution.py
+++ b/solution.py
@@ -148,6 +148,13 @@
     return value, (up + value * (2.0 - up)) * tangent
 
 
+def activate_hidden(y, tangent):
+    up = 1.0 + jnp.tanh(y)
+    value = (y * up).astype(BF16)
+    up = up.astype(BF16)
+    return value, (up + value * (2.0 - up)) * tangent.astype(BF16)
+
+
 def pair_step(packed, own_tab, tab, chunks, n, left_tab, right_tab, w_mids, w_lasts, w_radials, w_out,
               hot_own, hot_par, quant, acc_own, acc_par, width):
     nb = 8
@@ -191,12 +198,12 @@
         radials = jnp.dot(w_radials[...], jnp.concatenate(radials, 0).astype(BF16), preferred_element_type=F32)
         yield
         quarter = lambda x, half: x[64 * half:64 * half + 64]
-        now = [activate(g + quarter(radials, half)[:, 0:256], quarter(radials, half)[:, 256:512]) for half, g in enumerate(gathered)]
-        for w in (w_mids, w_lasts):
-            stack = jnp.concatenate([jnp.concatenate(pair, 1).astype(BF16) for pair in now], 0)
+        now = [activate_hidden(g + quarter(radials, half)[:, 0:256], quarter(radials, half)[:, 256:512]) for half, g in enumerate(gathered)]
+        for w, act in ((w_mids, activate_hidden), (w_lasts, activate)):
+            stack = jnp.concatenate([jnp.concatenate(pair, 1) for pair in now], 0)
             mixed = jnp.dot(w[...], stack, preferred_element_type=F32)
             yield
-            now = [activate(quarter(mixed, half)[:, 0:256], quarter(mixed, half)[:, 256:512]) for half in range(HALVES)]
+            now = [act(quarter(mixed, half)[:, 0:256], quarter(mixed, half)[:, 256:512]) for half in range(HALVES)]
         reads = [jnp.sum(value * w_out, 0, keepdims=True) for value, _ in now]
         slopes = [jnp.sum(slope * w_out, 0, keepdims=True) for _, slope in now]
         yield
@@ -328,6 +335,7 @@
     w_out = weights(radial, mid, last, out, w_mids, w_lasts, w_radials)
     gstand = compact(one, two, mask, own_tab, ghost_tab, chunks, gchunks, words, live, ranks, gpacked)
     acc_gho[...] = jnp.zeros_like(acc_gho)
+    rest = trips(stand[...], FEW)
     gstep = pair_step(gpacked, own_tab, ghost_tab, chunks, gchunks, left_tab, gtable, w_mids, w_lasts, w_radials, w_out,
                       hot_own, hot_par, quant, acc_own, acc_gho, GHOSTLY)
     lax.fori_loop(0, trips(gstand, GHOSTLY), gstep, 0)
@@ -338,7 +346,7 @@
     step = pair_step(packed, own_tab, own_tab, chunks, chunks, left_tab, right_tab, w_mids, w_lasts, w_radials, w_out,
                      hot_own, hot_par, quant, acc_own, acc_loc, FEW)
     stores = move((force,), (force_out,), out_sem)
-    lax.fori_loop((EARLY + LATE) // FEW, trips(stand[...], FEW), step, 0)
+    lax.fori_loop((EARLY + LATE) // FEW, rest, step, 0)
     finish(stores + move((acc_own, acc_loc), (acc_own_out, acc_loc_out), last_sem))
 
 

time: 38.9 us -> 38.7 us (level)
  no operation moved by 1% of the time
where the time goes in v7:
time: 38.7 us; the launch traced here: 38.3 us
  Pallas kernels  37.6 us (97%)
  between operations  0.66 us (2%)
    pallas_call x1, Pallas kernels, on_device(): pl.pallas_call(offer_kernel, name='offer', out_shape=made, in_specs=[HBM]...  16.2 us
    pallas_call x1, Pallas kernels, on_device(): pl.pallas_call(home_kernel, name='home', out_shape=made, in_specs=[HBM] *...  13.5 us
    pallas_call x1, Pallas kernels, on_device(): pl.pallas_call(pairs_kernel, name='pairs', out_shape=made, in_specs=[HBM]...  6.27 us
    pallas_call x1, Pallas kernels, on_device(): pl.pallas_call(join_kernel, name='join', out_shape=made, in_specs=[HBM] *...  1.7 us

profile of v7, /device:TPU:1, one launch (start us, length us, event | category | flops | bytes accessed | tf_op | source)
XLA Modules:
  0.0 38.3 jit_solution(6601229923960786026)
XLA Ops:
  0.6 16.2 %offer.1 = (f32[8,512]{1,0:T(8,128)}, bf16[128,256]{1,0:T(8,128)(2,1)}, bf16[128,256]{1,0:T(8,128)(2,1)}, bf16[7,72,256]{2,1,0:T(8,128)(2,1)}, s32[160,128]{1,0:...) custom-call(f32[3,512]{1,0:T(4,128)} %pos_hbm.1, bf16[64,512]{1,0:T(8,128)(2,1)} %feat_hbm.1, ...), custom_call_target="tpu_custom_call" | custom-call | tf_op jit(solution)/shard_map/offer/pallas_call | solution.py:427
  16.8 6.3 %pairs.1 = (f32[32,64]{1,0:T(8,128)}, f32[32,64]{1,0:T(8,128)}, f32[7,8,256]{2,1,0:T(8,128)}) custom-call(f32[8,512]{1,0:T(8,128)} %get-tuple-element.18.own_hbm, bf16[128,256]{1,0:T(8,128)(2,1)} %get-tuple-element.19.left_hbm, bf16[128,256]{1,0:T(8,128)(2,1)} %get-tuple-element.20.right_hbm, bf16[7,72,256]{2,1,0:T(8,128)(2,1)} %get-tuple-element.22.ghost_hbm, ...), custom_call_target="tpu_custom_call" | custom-call | tf_op jit(solution)/shard_map/pairs/pallas_call | solution.py:441
  23.1 13.5 %home.1 = (f32[32,64]{1,0:T(8,128)}, f32[32,64]{1,0:T(8,128)}, f32[7,8,256]{2,1,0:T(8,128)}) custom-call(f32[8,512]{1,0:T(8,128)} %get-tuple-element.18.own_hbm, bf16[128,256]{1,0:T(8,128)(2,1)} %get-tuple-element.19.left_hbm, bf16[128,256]{1,0:T(8,128)(2,1)} %get-tuple-element.20.right_hbm, s32[160,128]{1,0:T(8,128)} %get-tuple-element.21.packed_hbm, ...), custom_call_target="tpu_custom_call" | custom-call | tf_op jit(solution)/shard_map/home/pallas_call | solution.py:456
  36.6 1.7 %join.1 = (f32[3,512]{1,0:T(4,128)}, f32[1,512]{1,0:T(1,128)}) custom-call(f32[32,64]{1,0:T(8,128)} %get-tuple-element.29.acc_own_hbm, f32[32,64]{1,0:T(8,128)} %get-tuple-element.30.acc_loc_hbm, f32[7,8,256]{2,1,0:T(8,128)} %get-tuple-element.31.arrived_hbm, s32[1,256]{1,0:T(1,128)} %bitcast.25), custom_call_target="tpu_custom_call" | custom-call | tf_op jit(solution)/shard_map/join/pallas_call | solution.py:469

commit v8 on v7

--- a/solution.py
+++ b/solution.py
@@ -16,8 +16,8 @@
 F32, BF16, I32 = jnp.float32, jnp.bfloat16, jnp.int32
 LIVE = 128
 ROWS = 72
-EARLY = 8
-LATE = 8
+EARLY = 4
+LATE = 12
 HALVES = 4
 MANY = 4
 FEW = 2

time: 38.7 us -> 37.2 us (0.961)
  Pallas kernels: 37.6 us -> 36 us
    pallas_call x1, Pallas kernels: 13.5 us -> 12 us  [on_device(): pl.pallas_call(home_kernel, name='home', out_shape=made, in_specs=[HBM] *...]
where the time goes in v8:
time: 37.2 us; the launch traced here: 36.6 us
  Pallas kernels  36 us (97%)
  between operations  0.66 us (2%)
    pallas_call x1, Pallas kernels, on_device(): pl.pallas_call(offer_kernel, name='offer', out_shape=made, in_specs=[HBM]...  16 us
    pallas_call x1, Pallas kernels, on_device(): pl.pallas_call(home_kernel, name='home', out_shape=made, in_specs=[HBM] *...  12 us
    pallas_call x1, Pallas kernels, on_device(): pl.pallas_call(pairs_kernel, name='pairs', out_shape=made, in_specs=[HBM]...  6.27 us
    pallas_call x1, Pallas kernels, on_device(): pl.pallas_call(join_kernel, name='join', out_shape=made, in_specs=[HBM] *...  1.7 us

profile of v8, /device:TPU:1, one launch (start us, length us, event | category | flops | bytes accessed | tf_op | source)
XLA Modules:
  0.0 36.6 jit_solution(16197436738636528469)
XLA Ops:
  0.6 16.0 %offer.1 = (f32[8,512]{1,0:T(8,128)}, bf16[128,256]{1,0:T(8,128)(2,1)}, bf16[128,256]{1,0:T(8,128)(2,1)}, bf16[7,72,256]{2,1,0:T(8,128)(2,1)}, s32[160,128]{1,0:...) custom-call(f32[3,512]{1,0:T(4,128)} %pos_hbm.1, bf16[64,512]{1,0:T(8,128)(2,1)} %feat_hbm.1, ...), custom_call_target="tpu_custom_call" | custom-call | tf_op jit(solution)/shard_map/offer/pallas_call | solution.py:427
  16.7 6.3 %pairs.1 = (f32[32,64]{1,0:T(8,128)}, f32[32,64]{1,0:T(8,128)}, f32[7,8,256]{2,1,0:T(8,128)}) custom-call(f32[8,512]{1,0:T(8,128)} %get-tuple-element.18.own_hbm, bf16[128,256]{1,0:T(8,128)(2,1)} %get-tuple-element.19.left_hbm, bf16[128,256]{1,0:T(8,128)(2,1)} %get-tuple-element.20.right_hbm, bf16[7,72,256]{2,1,0:T(8,128)(2,1)} %get-tuple-element.22.ghost_hbm, ...), custom_call_target="tpu_custom_call" | custom-call | tf_op jit(solution)/shard_map/pairs/pallas_call | solution.py:441
  23.0 12.0 %home.1 = (f32[32,64]{1,0:T(8,128)}, f32[32,64]{1,0:T(8,128)}, f32[7,8,256]{2,1,0:T(8,128)}) custom-call(f32[8,512]{1,0:T(8,128)} %get-tuple-element.18.own_hbm, bf16[128,256]{1,0:T(8,128)(2,1)} %get-tuple-element.19.left_hbm, bf16[128,256]{1,0:T(8,128)(2,1)} %get-tuple-element.20.right_hbm, s32[160,128]{1,0:T(8,128)} %get-tuple-element.21.packed_hbm, ...), custom_call_target="tpu_custom_call" | custom-call | tf_op jit(solution)/shard_map/home/pallas_call | solution.py:456
  34.9 1.7 %join.1 = (f32[3,512]{1,0:T(4,128)}, f32[1,512]{1,0:T(1,128)}) custom-call(f32[32,64]{1,0:T(8,128)} %get-tuple-element.29.acc_own_hbm, f32[32,64]{1,0:T(8,128)} %get-tuple-element.30.acc_loc_hbm, f32[7,8,256]{2,1,0:T(8,128)} %get-tuple-element.31.arrived_hbm, s32[1,256]{1,0:T(1,128)} %bitcast.25), custom_call_target="tpu_custom_call" | custom-call | tf_op jit(solution)/shard_map/join/pallas_call | solution.py:469
